TPU v7x, 128 devices: a whole 4x4x4 slice. The times are simulated.
128 devices in a mesh: ctx: 64 (over x_lo, y, z, core), head: 2 (over x_hi).
Axes of the slice: x: 4 (x_hi: 2, x_lo: 2; x = x_hi * 2 + x_lo), y: 4, z: 4, core: 2. Of those that a mesh axis runs over, the one named last changes fastest.
Arguments:
- queries: bfloat16 [32768, 1024], P(('ctx', 'head')), may hold values from -9 to 9
- keys_in: bfloat16 [32768, 1024], P(('ctx', 'head')), may hold values from -9 to 9
- values: bfloat16 [32768, 1024], P(('ctx', 'head')), may hold values from -6 to 6
- d_out: bfloat16 [32768, 1024], P(('ctx', 'head')), may hold values from -6 to 6
- pair_blocks: int32 [512, 16], replicated, may hold values from 0 to 511, as said below
- pair_count: int32 [512], replicated, may hold values from 1 to 16, as said below
Outputs:
- d_queries: bfloat16 [32768, 1024], P(('ctx', 'head'))
- d_keys: bfloat16 [32768, 1024], P(('ctx', 'head'))
- d_values: bfloat16 [32768, 1024], P(('ctx', 'head'))
Inputs may be any that keep to these rules, and one draw needn't show every extreme that they name: `pair_blocks`: entry 0 of row b is b itself; every entry of row b is a block of a person within 2 persons of the person of block b (a person's tokens are 512 in a row). Entries may repeat. Only the first pair_count[b] entries of row b are listed.
All inputs are finite; a program needn't handle non-finite values.
Results may differ from a plain program's by a relative error of at most 0.012.
The roundings to bfloat16 on the way count: a program that leaves them out, or rounds other values in their place, can miss the bound.
Values may be sent and summed in bfloat16 or wider, within the bound.
A program may use at most 192 MiB of HBM per device.

v0:
```python
import jax
import jax.numpy as jnp
from jax import lax
from jax.sharding import PartitionSpec as P

HEAD_DIM = 64
BLOCK = 64
REACH = 2


masked_value = -1e30


def shifted(shard, axis, by):
    peers = lax.axis_size(axis)
    pairs = [(i, i + by) for i in range(peers) if 0 <= i + by < peers]
    return lax.ppermute(shard, axis, pairs)


def expand_mask(block_mask, block_rows):
    count_rows, count_cols = block_mask.shape
    widened = jnp.broadcast_to(
        block_mask[:, None, :, None], (count_rows, block_rows, count_cols, block_rows)
    )
    return widened.reshape(count_rows * block_rows, count_cols * block_rows)


def block_listing(pair_blocks, pair_count, first_query, query_blocks, first_key, key_blocks):
    lists = lax.dynamic_slice_in_dim(pair_blocks, first_query, query_blocks, 0)
    counts = lax.dynamic_slice_in_dim(pair_count, first_query, query_blocks, 0)
    live_slots = jnp.arange(lists.shape[1], dtype=jnp.int32)[None, :] < counts[:, None]
    wanted = first_key + jnp.arange(key_blocks, dtype=jnp.int32)
    return jnp.any((lists[:, :, None] == wanted[None, None, :]) & live_slots[:, :, None], axis=1)


def masked_scores(query_heads, key_heads, token_mask, score_scale):
    product = jnp.einsum("qhd,khd->hqk", query_heads, key_heads, preferred_element_type=jnp.float32)
    return jnp.where(token_mask[None], product * score_scale, masked_value)


def score_grads(probs, dout_heads, value_heads, row_delta):
    d_probs = jnp.einsum(
        "qhd,khd->hqk", dout_heads, value_heads, preferred_element_type=jnp.float32
    )
    return (probs * (d_probs - row_delta[:, :, None])).astype(jnp.bfloat16)


def key_value_grads(d_scores, probs, query_heads, dout_heads):
    key_part = jnp.einsum("hqk,qhd->khd", d_scores, query_heads, preferred_element_type=jnp.float32)
    value_part = jnp.einsum(
        "hqk,qhd->khd", probs.astype(jnp.bfloat16), dout_heads, preferred_element_type=jnp.float32
    )
    return jnp.stack([key_part, value_part]).astype(jnp.bfloat16)


def widen_part(rounded):
    return lax.optimization_barrier(rounded).astype(jnp.float32)


def on_device(queries, keys_in, values, d_out, pair_blocks, pair_count):
    entering = jnp.stack([queries, keys_in, values, d_out])
    head_local = lax.all_to_all(entering, "head", split_axis=2, concat_axis=1, tiled=True)
    frames = head_local.shape[1]
    feature_cols = head_local.shape[2]
    heads_dev = feature_cols // HEAD_DIM
    blocks_dev = frames // BLOCK
    window_span = 2 * REACH + 1
    score_scale = HEAD_DIM ** (-0.5)
    position = lax.axis_index("ctx")

    def split_heads(matrix):
        return matrix.reshape(frames, heads_dev, HEAD_DIM)

    query_heads = split_heads(head_local[0])
    dout_heads = split_heads(head_local[3])
    window_mask = block_listing(
        pair_blocks,
        pair_count,
        position * blocks_dev,
        blocks_dev,
        (position - REACH) * blocks_dev,
        window_span * blocks_dev,
    )
    key_pair = head_local[1:3]
    remote_tiles = {0: key_pair}
    for direction in (1, -1):
        current = key_pair
        for stride in range(1, REACH + 1):
            current = shifted(current, "ctx", direction)
            remote_tiles[-direction * stride] = current
    offsets = [0]
    for stride in range(1, REACH + 1):
        offsets = offsets + [-stride, stride]
    tile_masks = {}
    for offset in offsets:
        column = (offset + REACH) * blocks_dev
        tile_masks[offset] = expand_mask(window_mask[:, column : column + blocks_dev], BLOCK)
    row_top = jnp.full((heads_dev, frames), masked_value, jnp.float32)
    row_total = jnp.zeros((heads_dev, frames), jnp.float32)
    tile_scores = {}
    for offset in offsets:
        scores = masked_scores(
            query_heads, split_heads(remote_tiles[offset][0]), tile_masks[offset], score_scale
        )
        tile_scores[offset] = scores
        new_top = jnp.maximum(row_top, jnp.max(scores, axis=-1))
        kept = jnp.where(tile_masks[offset][None], jnp.exp(scores - new_top[:, :, None]), 0.0)
        row_total = row_total * jnp.exp(row_top - new_top) + jnp.sum(kept, axis=-1)
        row_top = new_top
    log_total = row_top + jnp.log(row_total)
    attention = jnp.zeros((frames, heads_dev, HEAD_DIM), jnp.float32)
    tile_probs = {}
    for offset in offsets:
        probs = jnp.where(
            tile_masks[offset][None], jnp.exp(tile_scores[offset] - log_total[:, :, None]), 0.0
        )
        tile_probs[offset] = probs
        attention = attention + jnp.einsum(
            "hqk,khd->qhd",
            probs.astype(jnp.bfloat16),
            split_heads(remote_tiles[offset][1]),
            preferred_element_type=jnp.float32,
        )
    row_delta = jnp.sum(dout_heads.astype(jnp.float32) * attention, axis=-1).T
    query_grad = jnp.zeros((frames, heads_dev, HEAD_DIM), jnp.float32)
    tile_parts = {}
    for offset in offsets:
        key_heads = split_heads(remote_tiles[offset][0])
        d_scores = score_grads(
            tile_probs[offset], dout_heads, split_heads(remote_tiles[offset][1]), row_delta
        )
        query_grad = query_grad + jnp.einsum(
            "hqk,khd->qhd", d_scores, key_heads, preferred_element_type=jnp.float32
        )
        tile_parts[offset] = key_value_grads(d_scores, tile_probs[offset], query_heads, dout_heads)
    collected = widen_part(tile_parts[0])
    for offset in offsets[1:]:
        arrived = shifted(tile_parts[offset], "ctx", offset)
        collected = collected + arrived.astype(jnp.float32)
    query_out = (query_grad * score_scale).astype(jnp.bfloat16).reshape(frames, feature_cols)
    key_out = (collected[0] * score_scale).astype(jnp.bfloat16).reshape(frames, feature_cols)
    value_out = collected[1].astype(jnp.bfloat16).reshape(frames, feature_cols)
    leaving = lax.all_to_all(
        jnp.stack([query_out, key_out, value_out]), "head", split_axis=1, concat_axis=2, tiled=True
    )
    return (leaving[0], leaving[1], leaving[2])


def solution(mesh):
    placed = (
        P(("ctx", "head"), None),
        P(("ctx", "head"), None),
        P(("ctx", "head"), None),
        P(("ctx", "head"), None),
        P(),
        P(),
    )
    return jax.shard_map(
        on_device,
        mesh=mesh,
        in_specs=placed,
        out_specs=(P(("ctx", "head"), None), P(("ctx", "head"), None), P(("ctx", "head"), None)),
        check_vma=False,
    )
```

profile of v0, /device:TPU:121, one launch (start us, length us, event | category | flops | bytes accessed | tf_op | source)
XLA Modules:
  0.0 277.8 jit_solution(14616400120939298782)
XLA Ops:
  0.6 1.8 pad_maximum_fusion
  2.4 2.6 copy.108
  5.0 4.0 %all-to-all-start = ((bf16[4,256,1024]{1,0,2:T(4,128)(2,1)}), bf16[4,256,1024]{1,0,2:T(4,128)(2,1)S(1)}, u32[]{:S(2)}, u32[]{:S(2)}) async-start(bf16[4,256,1024]{1,0,2:T(4,128)(2,1)} %copy.108), calls=%async_computation | async-start | bytes 4194304 | tf_op jit(solution)/shard_map/all_to_all | solution.py:62
  10.0 24.4 %all-to-all-done = bf16[4,256,1024]{1,0,2:T(4,128)(2,1)S(1)} async-done(((bf16[4,256,1024]{1,0,2:T(4,128)(2,1)}), bf16[4,256,1024]{1,0,2:T(4,128)(2,1)S(1)}, u32[]{:S(2)}, u32[]{:S(2)}) %all-to-all-start) | async-done | bytes 2097184 | tf_op jit(solution)/shard_map/all_to_all | solution.py:62
  34.5 1.3 copy-done.5
  35.8 3.7 %copy.176 = bf16[4,256,2,512]{1,2,3,0:T(2,128)(2,1)S(1)} copy(bf16[4,256,2,512]{1,0,3,2:T(4,128)(2,1)} %bitcast.163) | data formatting | bytes 4194304 | tf_op jit(solution)/shard_map/all_to_all | solution.py:62
  40.3 1.5 slice.97
  41.8 3.8 %collective-permute-start.1 = (bf16[2,512,512]{1,2,0:T(8,128)(2,1)}, bf16[2,512,512]{1,2,0:T(8,128)(2,1)}, u32[]{:S(2)}, u32[]{:S(2)}) collective-permute-start(bf16[2,512,512]{1,2,0:T(8,128)(2,1)} %slice.97), channel_id=1, source_target_pairs={{2,0},{4,2},{6,4},{8,6},{10,8},{12,10},{14,12},{16,14},{18,16},{20... | collective-permute-start | bytes 3145736 | tf_op jit(solution)/shard_map/ppermute | solution.py:17
  45.7 6.2 %collective-permute-start = (bf16[2,512,512]{1,2,0:T(8,128)(2,1)}, bf16[2,512,512]{1,2,0:T(8,128)(2,1)}, u32[]{:S(2)}, u32[]{:S(2)}) collective-permute-start(bf16[2,512,512]{1,2,0:T(8,128)(2,1)} %slice.97), channel_id=1, source_target_pairs={{0,2},{2,4},{4,6},{6,8},{8,10},{10,12},{12,14},{14,16},{16,18},{18... | collective-permute-start | bytes 3145736 | tf_op jit(solution)/shard_map/ppermute | solution.py:17
  56.0 1.8 broadcast_in_dim.150
  58.9 1.8 broadcast_in_dim.145
  60.7 2.4 fusion.44
  63.1 1.4 reshape_squeeze.52
  64.5 1.4 reshape_squeeze.47
  65.9 1.4 reshape_squeeze.46
  67.2 2.2 reshape_squeeze.53
  69.4 1.5 fusion.5
  70.9 1.9 collective-permute-start.3
  72.8 1.3 fusion.46
  74.1 8.1 %collective-permute-start.2 = (bf16[2,512,512]{1,2,0:T(8,128)(2,1)}, bf16[2,512,512]{1,2,0:T(8,128)(2,1)S(1)}, u32[]{:S(2)}, u32[]{:S(2)}) collective-permute-start(bf16[2,512,512]{1,2,0:T(8,128)(2,1)} %collective-permute-done), channel_id=1, source_target_pairs={{0,2},{2,4},{4,6},{6,8},{8,10},{10,12},{12,14},{14,16},{16,18},{18... | collective-permute-start | bytes 3145736 | tf_op jit(solution)/shard_map/ppermute | solution.py:17
  82.3 1.3 fusion.47
  83.5 1.5 fusion.7
  85.0 1.5 fusion.6
  86.5 4.9 %collective-permute-done.3 = bf16[2,512,512]{1,2,0:T(8,128)(2,1)S(1)} collective-permute-done((bf16[2,512,512]{1,2,0:T(8,128)(2,1)}, bf16[2,512,512]{1,2,0:T(8,128)(2,1)S(1)}, u32[]{:S(2)}, u32[]{:S(2)}) %collective-permute-start.3) | collective-permute-done | bytes 1048608 | tf_op jit(solution)/shard_map/ppermute | solution.py:17
  91.5 4.7 %fusion.9 = (f32[8,512]{1,0:T(8,128)S(1)}, f32[8,512,512]{1,2,0:T(8,128)}) fusion(pred[512,512]{0,1:T(8,128)(4,1)S(1)} %broadcast_in_dim.159, bf16[512,8,64]{0,2,1:T(8,128)(2,1)S(1)} %reshape_squeeze.47, bf16[512,8,64]{0,2,1:T(8,128)(2,1)S(1)} %bitcast.170), kind=kOutput, calls=%fused_computation.29 | convolution fusion | flops 274722816 | bytes 9715712 | tf_op jit(solution)/shard_map/qhd,khd->hqk/dot_general | solution.py:37
  96.3 4.7 %fusion.8 = (f32[8,512]{1,0:T(8,128)S(1)}, f32[8,512,512]{1,2,0:T(8,128)}) fusion(pred[512,512]{0,1:T(8,128)(4,1)S(1)} %broadcast_in_dim.156, bf16[512,8,64]{0,2,1:T(8,128)(2,1)S(1)} %reshape_squeeze.47, bf16[512,8,64]{0,2,1:T(8,128)(2,1)S(1)} %bitcast.164), kind=kOutput, calls=%fused_computation.28 | convolution fusion | flops 274722816 | bytes 9715712 | tf_op jit(solution)/shard_map/qhd,khd->hqk/dot_general | solution.py:37
  101.1 2.5 select_reduce_fusion.4
  103.6 7.9 %select_reduce_fusion = (f32[8,512]{1,0:T(8,128)S(1)}, f32[8,512]{1,0:T(8,128)S(1)}) fusion(f32[8,512,512]{1,2,0:T(8,128)} %get-tuple-element.29, f32[8,512]{1,0:T(8,128)S(1)} %get-tuple-element.3, pred[512,512]{0,1:T(8,128)(4,1)S(1)} %broadcast_in_dim.159, f32[8,512]{1,0:T(8,128)S(1)} %get-tuple-element.4, f32[8,512,512]{1,2,0:T(8,128)} %get-tuple-element.31, ...), kind=kLoop, calls=%fused_computation.10 | loop fusion | flops 20963328 | bytes 17367040 | tf_op jit(solution)/shard_map/reduce_sum | solution.py:108
  111.5 4.0 %select_reduce_fusion.2 = (f32[8,512]{1,0:T(8,128)S(1)}, f32[8,512]{1,0:T(8,128)S(1)}) fusion(f32[8,512,512]{1,2,0:T(8,128)S(1)} %get-tuple-element.33, f32[8,512]{1,0:T(8,128)S(1)} %get-tuple-element.5, pred[512,512]{0,1:T(8,128)(4,1)S(1)} %broadcast_in_dim.153, f32[8,512]{1,0:T(8,128)S(1)} %get-tuple-element.6, f32[8,512,512]{1,2,0:T(8,128)S(1)} %get-tuple-element.35, ...), kind=kLoop, calls=%fused_computation.12 | loop fusion | flops 20963328 | bytes 17367040 | tf_op jit(solution)/shard_map/reduce_sum | solution.py:108
  115.5 6.5 %fusion.26 = bf16[1,512,8,64]{1,3,2,0:T(8,128)(2,1)} fusion(bf16[512,8,64]{0,2,1:T(8,128)(2,1)S(1)} %reshape_squeeze.52, f32[8,512,512]{1,2,0:T(8,128)} %get-tuple-element.29, f32[8,512]{1,0:T(8,128)S(1)} %log_add_fusion, pred[512,512]{0,1:T(8,128)(4,1)S(1)} %broadcast_in_dim.159), kind=kOutput, calls=%fused_computation.66 | convolution fusion | flops 279183360 | bytes 9715712 | tf_op jit(solution)/shard_map/hqk,qhd->khd/dot_general | solution.py:50
  122.0 6.5 %fusion.24 = bf16[1,512,8,64]{1,3,2,0:T(8,128)(2,1)} fusion(bf16[512,8,64]{0,2,1:T(8,128)(2,1)S(1)} %reshape_squeeze.52, f32[8,512,512]{1,2,0:T(8,128)} %get-tuple-element.31, f32[8,512]{1,0:T(8,128)S(1)} %log_add_fusion, pred[512,512]{0,1:T(8,128)(4,1)S(1)} %broadcast_in_dim.156), kind=kOutput, calls=%fused_computation.64 | convolution fusion | flops 279183360 | bytes 9715712 | tf_op jit(solution)/shard_map/hqk,qhd->khd/dot_general | solution.py:50
  128.5 5.8 %fusion.36 = f32[8,64,512]{2,1,0:T(8,128)S(1)} fusion(bf16[512,8,64]{0,2,1:T(8,128)(2,1)S(1)} %bitcast.185, f32[8,512,512]{1,2,0:T(8,128)} %get-tuple-element.29, f32[8,512]{1,0:T(8,128)S(1)} %log_add_fusion, pred[512,512]{0,1:T(8,128)(4,1)S(1)} %broadcast_in_dim.159), kind=kOutput, calls=%fused_computation.82 | convolution fusion | flops 278921216 | bytes 10240000 | tf_op jit(solution)/shard_map/hqk,khd->qhd/dot_general | solution.py:118
  134.3 2.6 fusion.39
  136.8 2.4 convolution_add_fusion.5
  139.3 2.4 convolution_add_fusion.4
  141.8 5.9 %fusion.16 = f32[512,8]{0,1:T(8,128)S(1)} fusion(f32[8,64,512]{2,1,0:T(8,128)S(1)} %fusion.36, f32[8,64,512]{2,1,0:T(8,128)S(1)} %convolution_add_fusion.4, bf16[512,8,64]{0,2,1:T(8,128)(2,1)S(1)} %bitcast.187, bf16[512,8,64]{0,2,1:T(8,128)(2,1)S(1)} %reshape_squeeze.52, f32[8,512,512]{1,2,0:T(8,128)} %get-tuple-element.31, f32[8,512]{1,0:T(8,128)S(1)} %log_add_fusion, ...), kind=kOutput, calls=%fused_computation.56 | convolution fusion | flops 280227840 | bytes 11829248 | tf_op jit(solution)/shard_map/hqk,khd->qhd/dot_general | solution.py:118
  147.7 6.8 %multiply_convert_fusion = bf16[8,512,512]{1,2,0:T(8,128)(2,1)} fusion(f32[8,512,512]{1,2,0:T(8,128)} %get-tuple-element.29, f32[8,512]{1,0:T(8,128)S(1)} %bitcast.193, f32[8,512]{1,0:T(8,128)S(1)} %log_add_fusion, pred[512,512]{0,1:T(8,128)(4,1)S(1)} %broadcast_in_dim.159, bf16[512,8,64]{0,2,1:T(8,128)(2,1)S(1)} %reshape_squeeze.52, ...), kind=kOutput, calls=%fused_computation | convolution fusion | flops 283115520 | bytes 13926400 | tf_op jit(solution)/shard_map/qhd,khd->hqk/dot_general | solution.py:42
  154.5 6.8 %multiply_convert_fusion.1 = bf16[8,512,512]{1,2,0:T(8,128)(2,1)} fusion(f32[8,512,512]{1,2,0:T(8,128)} %get-tuple-element.31, f32[8,512]{1,0:T(8,128)S(1)} %bitcast.194, f32[8,512]{1,0:T(8,128)S(1)} %log_add_fusion, pred[512,512]{0,1:T(8,128)(4,1)S(1)} %broadcast_in_dim.156, bf16[512,8,64]{0,2,1:T(8,128)(2,1)S(1)} %reshape_squeeze.52, ...), kind=kOutput, calls=%fused_computation.1 | convolution fusion | flops 283115520 | bytes 13926400 | tf_op jit(solution)/shard_map/qhd,khd->hqk/dot_general | solution.py:42
  161.3 3.3 %fusion.22 = bf16[1,512,8,64]{1,3,2,0:T(8,128)(2,1)} fusion(bf16[512,8,64]{0,2,1:T(8,128)(2,1)S(1)} %reshape_squeeze.52, f32[8,512,512]{1,2,0:T(8,128)S(1)} %get-tuple-element.33, f32[8,512]{1,0:T(8,128)S(1)} %log_add_fusion, pred[512,512]{0,1:T(8,128)(4,1)S(1)} %broadcast_in_dim.153), kind=kOutput, calls=%fused_computation.62 | convolution fusion | flops 279183360 | bytes 9715712 | tf_op jit(solution)/shard_map/hqk,qhd->khd/dot_general | solution.py:50
  164.6 4.8 %multiply_convert_fusion.2 = bf16[8,512,512]{1,2,0:T(8,128)(2,1)} fusion(f32[8,512,512]{1,2,0:T(8,128)S(1)} %get-tuple-element.33, f32[8,512]{1,0:T(8,128)S(1)} %bitcast.195, f32[8,512]{1,0:T(8,128)S(1)} %log_add_fusion, pred[512,512]{0,1:T(8,128)(4,1)S(1)} %broadcast_in_dim.153, bf16[512,8,64]{0,2,1:T(8,128)(2,1)S(1)} %reshape_squeeze.52, ...), kind=kOutput, calls=%fused_computation.2 | convolution fusion | flops 283115520 | bytes 13926400 | tf_op jit(solution)/shard_map/qhd,khd->hqk/dot_general | solution.py:42
  169.4 3.3 %fusion.20 = bf16[1,512,8,64]{1,3,2,0:T(8,128)(2,1)} fusion(bf16[512,8,64]{0,2,1:T(8,128)(2,1)S(1)} %reshape_squeeze.52, f32[8,512,512]{1,2,0:T(8,128)S(1)} %get-tuple-element.35, f32[8,512]{1,0:T(8,128)S(1)} %log_add_fusion, pred[512,512]{0,1:T(8,128)(4,1)S(1)} %broadcast_in_dim.150), kind=kOutput, calls=%fused_computation.60 | convolution fusion | flops 279183360 | bytes 9715712 | tf_op jit(solution)/shard_map/hqk,qhd->khd/dot_general | solution.py:50
  172.7 3.4 %multiply_convert_fusion.3 = bf16[8,512,512]{1,2,0:T(8,128)(2,1)S(1)} fusion(f32[8,512,512]{1,2,0:T(8,128)S(1)} %get-tuple-element.35, f32[8,512]{1,0:T(8,128)S(1)} %bitcast.196, f32[8,512]{1,0:T(8,128)S(1)} %log_add_fusion, pred[512,512]{0,1:T(8,128)(4,1)S(1)} %broadcast_in_dim.150, bf16[512,8,64]{0,2,1:T(8,128)(2,1)S(1)} %reshape_squeeze.52, ...), kind=kOutput, calls=%fused_computation.3 | convolution fusion | flops 283115520 | bytes 13926400 | tf_op jit(solution)/shard_map/qhd,khd->hqk/dot_general | solution.py:42
  176.1 2.5 fusion.18
  178.6 3.4 %multiply_convert_fusion.4 = bf16[8,512,512]{1,2,0:T(8,128)(2,1)S(1)} fusion(f32[8,512,512]{1,2,0:T(8,128)S(1)} %get-tuple-element.37, f32[8,512]{1,0:T(8,128)S(1)} %bitcast.197, f32[8,512]{1,0:T(8,128)S(1)} %log_add_fusion, pred[512,512]{0,1:T(8,128)(4,1)S(1)} %broadcast_in_dim.145, bf16[512,8,64]{0,2,1:T(8,128)(2,1)S(1)} %reshape_squeeze.52, ...), kind=kOutput, calls=%fused_computation.4 | convolution fusion | flops 283115520 | bytes 13926400 | tf_op jit(solution)/shard_map/qhd,khd->hqk/dot_general | solution.py:42
  182.1 1.4 fusion.17
  184.4 1.4 fusion.25
  185.8 1.1 pad_maximum_fusion.6
  186.8 1.9 collective-permute-start.7
  188.8 1.4 fusion.23
  190.2 1.1 pad_maximum_fusion.5
  191.3 3.6 %collective-permute-start.6 = (bf16[2,512,8,64]{1,3,2,0:T(8,128)(2,1)}, bf16[2,512,8,64]{1,3,2,0:T(8,128)(2,1)}, u32[]{:S(2)}, u32[]{:S(2)}) collective-permute-start(bf16[2,512,8,64]{1,3,2,0:T(8,128)(2,1)} %pad_maximum_fusion.5), channel_id=1, source_target_pairs={{4,0},{6,2},{8,4},{10,6},{12,8},{14,10},{16,12},{18,14},{20,16},{2... | collective-permute-start | bytes 3145736 | tf_op jit(solution)/shard_map/ppermute | solution.py:17
  194.9 1.4 fusion.21
  196.3 1.1 pad_maximum_fusion.4
  197.3 11.0 %collective-permute-start.5 = (bf16[2,512,8,64]{1,3,2,0:T(8,128)(2,1)}, bf16[2,512,8,64]{1,3,2,0:T(8,128)(2,1)}, u32[]{:S(2)}, u32[]{:S(2)}) collective-permute-start(bf16[2,512,8,64]{1,3,2,0:T(8,128)(2,1)} %pad_maximum_fusion.4), channel_id=1, source_target_pairs={{0,2},{2,4},{4,6},{6,8},{8,10},{10,12},{12,14},{14,16},{16,18},{18... | collective-permute-start | bytes 3145736 | tf_op jit(solution)/shard_map/ppermute | solution.py:17
  208.4 1.4 fusion.19
  209.8 1.1 pad_maximum_fusion.3
  210.9 1.9 collective-permute-start.4
  217.6 5.7 %collective-permute-done.5 = bf16[2,512,8,64]{1,3,2,0:T(8,128)(2,1)} collective-permute-done((bf16[2,512,8,64]{1,3,2,0:T(8,128)(2,1)}, bf16[2,512,8,64]{1,3,2,0:T(8,128)(2,1)}, u32[]{:S(2)}, u32[]{:S(2)}) %collective-permute-start.5) | collective-permute-done | bytes 1048608 | tf_op jit(solution)/shard_map/ppermute | solution.py:17
  223.3 10.5 %collective-permute-done.4 = bf16[2,512,8,64]{1,3,2,0:T(8,128)(2,1)} collective-permute-done((bf16[2,512,8,64]{1,3,2,0:T(8,128)(2,1)}, bf16[2,512,8,64]{1,3,2,0:T(8,128)(2,1)}, u32[]{:S(2)}, u32[]{:S(2)}) %collective-permute-start.4) | collective-permute-done | bytes 1048608 | tf_op jit(solution)/shard_map/ppermute | solution.py:17
  233.8 3.0 %convert_add_fusion = f32[2,512,8,64]{1,3,2,0:T(8,128)S(1)} fusion(bf16[2,512,8,64]{1,3,2,0:T(8,128)(2,1)} %collective-permute-done.7, bf16[2,512,8,64]{1,3,2,0:T(8,128)(2,1)} %collective-permute-done.6, bf16[2,512,8,64]{1,3,2,0:T(8,128)(2,1)} %collective-permute-done.5, bf16[2,512,8,64]{1,3,2,0:T(8,128)(2,1)} %collective-permute-done.4, ...), kind=kLoop, calls=%fused_computation.33 | loop fusion | flops 4718592 | bytes 7340032 | tf_op jit(solution)/shard_map/add | solution.py:139
  238.7 2.4 copy.142
  241.1 3.6 %pad_maximum_fusion.1 = bf16[3,512,512]{2,0,1:T(4,128)(2,1)S(1)} fusion(bf16[1,512,512]{2,0,1:T(2,128)(2,1)S(1)} %copy.143, bf16[1,512,512]{2,0,1:T(2,128)(2,1)S(1)} %copy.142, bf16[1,512,512]{2,0,1:T(2,128)(2,1)S(1)} %copy.141), kind=kLoop, calls=%fused_computation.31 | loop fusion | flops 4718592 | bytes 3145728 | tf_op jit(solution)/shard_map/stack | solution.py:144
  244.7 25.3 %all_to_all.30 = bf16[3,512,512]{2,0,1:T(4,128)(2,1)S(1)} all-to-all(bf16[3,512,512]{2,0,1:T(4,128)(2,1)S(1)} %pad_maximum_fusion.1), channel_id=1, replica_groups=mesh['ctx'=64,'head'=2] {'head'}, dimensions={1} | all-to-all | bytes 3145728 | tf_op jit(solution)/shard_map/all_to_all | solution.py:143
  270.0 2.2 fusion.43
  (81 shorter events, 19.7 us)
Async XLA Ops:
  0.6 8.4 %copy-start = (s32[512,16]{0,1:T(8,128)S(1)}, s32[512,16]{0,1:T(8,128)}, u32[]{:S(2)}) copy-start(s32[512,16]{0,1:T(8,128)} %param.10) | copy-start | bytes 98308
  5.0 29.4 %all-to-all-start = ((bf16[4,256,1024]{1,0,2:T(4,128)(2,1)}), bf16[4,256,1024]{1,0,2:T(4,128)(2,1)S(1)}, u32[]{:S(2)}, u32[]{:S(2)}) async-start(bf16[4,256,1024]{1,0,2:T(4,128)(2,1)} %copy.108), calls=%async_computation | async-start | bytes 4194304 | tf_op jit(solution)/shard_map/all_to_all | solution.py:62
  34.5 1.3 copy-start.5
  41.8 29.1 %collective-permute-start.1 = (bf16[2,512,512]{1,2,0:T(8,128)(2,1)}, bf16[2,512,512]{1,2,0:T(8,128)(2,1)}, u32[]{:S(2)}, u32[]{:S(2)}) collective-permute-start(bf16[2,512,512]{1,2,0:T(8,128)(2,1)} %slice.97), channel_id=1, source_target_pairs={{2,0},{4,2},{6,4},{8,6},{10,8},{12,10},{14,12},{16,14},{18,16},{20... | collective-permute-start | bytes 3145736 | tf_op jit(solution)/shard_map/ppermute | solution.py:17
  45.7 28.4 %collective-permute-start = (bf16[2,512,512]{1,2,0:T(8,128)(2,1)}, bf16[2,512,512]{1,2,0:T(8,128)(2,1)}, u32[]{:S(2)}, u32[]{:S(2)}) collective-permute-start(bf16[2,512,512]{1,2,0:T(8,128)(2,1)} %slice.97), channel_id=1, source_target_pairs={{0,2},{2,4},{4,6},{6,8},{8,10},{10,12},{12,14},{14,16},{16,18},{18... | collective-permute-start | bytes 3145736 | tf_op jit(solution)/shard_map/ppermute | solution.py:17
  70.9 20.5 %collective-permute-start.3 = (bf16[2,512,512]{1,2,0:T(8,128)(2,1)}, bf16[2,512,512]{1,2,0:T(8,128)(2,1)S(1)}, u32[]{:S(2)}, u32[]{:S(2)}) collective-permute-start(bf16[2,512,512]{1,2,0:T(8,128)(2,1)} %collective-permute-done.1), channel_id=1, source_target_pairs={{2,0},{4,2},{6,4},{8,6},{10,8},{12,10},{14,12},{16,14},{18,16},{20... | collective-permute-start | bytes 3145736 | tf_op jit(solution)/shard_map/ppermute | solution.py:17
  74.1 65.2 %copy-start.8 = (bf16[1,512,512]{1,2,0:T(8,128)(2,1)}, bf16[1,512,512]{1,2,0:T(8,128)(2,1)S(1)}, u32[]{:S(2)}) copy-start(bf16[1,512,512]{1,2,0:T(8,128)(2,1)S(1)} %get-tuple-element.16) | copy-start | bytes 1572868
  74.1 22.1 %collective-permute-start.2 = (bf16[2,512,512]{1,2,0:T(8,128)(2,1)}, bf16[2,512,512]{1,2,0:T(8,128)(2,1)S(1)}, u32[]{:S(2)}, u32[]{:S(2)}) collective-permute-start(bf16[2,512,512]{1,2,0:T(8,128)(2,1)} %collective-permute-done), channel_id=1, source_target_pairs={{0,2},{2,4},{4,6},{6,8},{8,10},{10,12},{12,14},{14,16},{16,18},{18... | collective-permute-start | bytes 3145736 | tf_op jit(solution)/shard_map/ppermute | solution.py:17
  83.5 53.3 %copy-start.10 = (bf16[1,512,512]{1,2,0:T(8,128)(2,1)}, bf16[1,512,512]{1,2,0:T(8,128)(2,1)S(1)}, u32[]{:S(2)}) copy-start(bf16[1,512,512]{1,2,0:T(8,128)(2,1)S(1)} %get-tuple-element.18) | copy-start | bytes 1572868
  91.5 37.0 %copy-start.12 = (bf16[1,512,512]{1,2,0:T(8,128)(2,1)}, bf16[1,512,512]{1,2,0:T(8,128)(2,1)S(1)}, u32[]{:S(2)}) copy-start(bf16[1,512,512]{1,2,0:T(8,128)(2,1)S(1)} %get-tuple-element.20) | copy-start | bytes 1572868
  96.3 45.4 %copy-start.13 = (bf16[1,512,512]{1,2,0:T(8,128)(2,1)}, bf16[1,512,512]{1,2,0:T(8,128)(2,1)S(1)}, u32[]{:S(2)}) copy-start(bf16[1,512,512]{1,2,0:T(8,128)(2,1)S(1)} %get-tuple-element.14) | copy-start | bytes 1572868
  128.5 5.8 %copy-start.6 = (bf16[512,8,64]{0,2,1:T(8,128)(2,1)S(1)}, bf16[512,8,64]{0,2,1:T(8,128)(2,1)}, u32[]{:S(2)}) copy-start(bf16[512,8,64]{0,2,1:T(8,128)(2,1)} %reshape_squeeze.53) | copy-start | bytes 1572868
  161.3 3.3 %copy-start.9 = (bf16[1,512,512]{1,2,0:T(8,128)(2,1)S(1)}, bf16[1,512,512]{1,2,0:T(8,128)(2,1)}, u32[]{:S(2)}) copy-start(bf16[1,512,512]{1,2,0:T(8,128)(2,1)} %copy-done.8) | copy-start | bytes 1572868
  169.4 3.3 %copy-start.11 = (bf16[1,512,512]{1,2,0:T(8,128)(2,1)S(1)}, bf16[1,512,512]{1,2,0:T(8,128)(2,1)}, u32[]{:S(2)}) copy-start(bf16[1,512,512]{1,2,0:T(8,128)(2,1)} %copy-done.10) | copy-start | bytes 1572868
  176.1 2.5 copy-start.7
  182.1 2.3 copy-start.3
  182.1 3.7 %copy-start.15 = (bf16[1,512,8,64]{1,3,2,0:T(8,128)(2,1)S(1)}, bf16[1,512,8,64]{1,3,2,0:T(8,128)(2,1)}, u32[]{:S(2)}) copy-start(bf16[1,512,8,64]{1,3,2,0:T(8,128)(2,1)} %fusion.26) | copy-start | bytes 1572868
  182.1 6.7 %copy-start.2 = (bf16[8,512,512]{1,2,0:T(8,128)(2,1)S(1)}, bf16[8,512,512]{1,2,0:T(8,128)(2,1)}, u32[]{:S(2)}) copy-start(bf16[8,512,512]{1,2,0:T(8,128)(2,1)} %multiply_convert_fusion.1) | copy-start | bytes 12582916
  183.5 6.7 %copy-start.14 = (bf16[1,512,8,64]{1,3,2,0:T(8,128)(2,1)S(1)}, bf16[1,512,8,64]{1,3,2,0:T(8,128)(2,1)}, u32[]{:S(2)}) copy-start(bf16[1,512,8,64]{1,3,2,0:T(8,128)(2,1)} %fusion.24) | copy-start | bytes 1572868
  184.4 10.5 %copy-start.4 = (bf16[8,512,512]{1,2,0:T(8,128)(2,1)S(1)}, bf16[8,512,512]{1,2,0:T(8,128)(2,1)}, u32[]{:S(2)}) copy-start(bf16[8,512,512]{1,2,0:T(8,128)(2,1)} %multiply_convert_fusion.2) | copy-start | bytes 12582916
  185.8 10.5 %copy-start.17 = (bf16[1,512,8,64]{1,3,2,0:T(8,128)(2,1)S(1)}, bf16[1,512,8,64]{1,3,2,0:T(8,128)(2,1)}, u32[]{:S(2)}) copy-start(bf16[1,512,8,64]{1,3,2,0:T(8,128)(2,1)} %fusion.22) | copy-start | bytes 1572868
  186.8 30.2 %collective-permute-start.7 = (bf16[2,512,8,64]{1,3,2,0:T(8,128)(2,1)}, bf16[2,512,8,64]{1,3,2,0:T(8,128)(2,1)}, u32[]{:S(2)}, u32[]{:S(2)}) collective-permute-start(bf16[2,512,8,64]{1,3,2,0:T(8,128)(2,1)} %pad_maximum_fusion.6), channel_id=1, source_target_pairs={{0,4},{2,6},{4,8},{6,10},{8,12},{10,14},{12,16},{14,18},{16,20},{1... | collective-permute-start | bytes 3145736 | tf_op jit(solution)/shard_map/ppermute | solution.py:17
  190.2 19.6 %copy-start.16 = (bf16[1,512,8,64]{1,3,2,0:T(8,128)(2,1)S(1)}, bf16[1,512,8,64]{1,3,2,0:T(8,128)(2,1)}, u32[]{:S(2)}) copy-start(bf16[1,512,8,64]{1,3,2,0:T(8,128)(2,1)} %fusion.20) | copy-start | bytes 1572868
  191.3 26.3 %collective-permute-start.6 = (bf16[2,512,8,64]{1,3,2,0:T(8,128)(2,1)}, bf16[2,512,8,64]{1,3,2,0:T(8,128)(2,1)}, u32[]{:S(2)}, u32[]{:S(2)}) collective-permute-start(bf16[2,512,8,64]{1,3,2,0:T(8,128)(2,1)} %pad_maximum_fusion.5), channel_id=1, source_target_pairs={{4,0},{6,2},{8,4},{10,6},{12,8},{14,10},{16,12},{18,14},{20,16},{2... | collective-permute-start | bytes 3145736 | tf_op jit(solution)/shard_map/ppermute | solution.py:17
  197.3 25.9 %collective-permute-start.5 = (bf16[2,512,8,64]{1,3,2,0:T(8,128)(2,1)}, bf16[2,512,8,64]{1,3,2,0:T(8,128)(2,1)}, u32[]{:S(2)}, u32[]{:S(2)}) collective-permute-start(bf16[2,512,8,64]{1,3,2,0:T(8,128)(2,1)} %pad_maximum_fusion.4), channel_id=1, source_target_pairs={{0,2},{2,4},{4,6},{6,8},{8,10},{10,12},{12,14},{14,16},{16,18},{18... | collective-permute-start | bytes 3145736 | tf_op jit(solution)/shard_map/ppermute | solution.py:17
  210.9 22.9 %collective-permute-start.4 = (bf16[2,512,8,64]{1,3,2,0:T(8,128)(2,1)}, bf16[2,512,8,64]{1,3,2,0:T(8,128)(2,1)}, u32[]{:S(2)}, u32[]{:S(2)}) collective-permute-start(bf16[2,512,8,64]{1,3,2,0:T(8,128)(2,1)} %pad_maximum_fusion.3), channel_id=1, source_target_pairs={{2,0},{4,2},{6,4},{8,6},{10,8},{12,10},{14,12},{16,14},{18,16},{20... | collective-permute-start | bytes 3145736 | tf_op jit(solution)/shard_map/ppermute | solution.py:17
  241.1 36.2 %copy-start.1 = (s32[512,16]{0,1:T(8,128)S(1)}, s32[512,16]{0,1:T(8,128)}, u32[]{:S(2)}) copy-start(s32[512,16]{0,1:T(8,128)} %param.10) | copy-start | bytes 98308
where the time goes:
time: 282 us; the launch traced here: 278 us
  matrix products  91.4 us (32%)
  waiting for transfers between devices  46.1 us (16%)
  local copies, waits for them, and re-layouts  42.5 us (15%)
  starting transfers between devices  42.5 us (15%)
  other arithmetic  28.3 us (10%)
  blocking collectives  25.3 us (9%)
    ppermute x8, starting transfers between devices, shifted(): return lax.ppermute(shard, axis, pairs)  38.5 us
    all_to_all x1, blocking collectives, on_device(): lax.all_to_all(jnp.stack([query_out, key_out, value_out]), 'head', split_...  25.3 us
    dot_general x5, matrix products, score_grads(): jnp.einsum('qhd,khd->hqk', dout_heads, value_heads, preferred_element_typ...  25.3 us
    all_to_all x1, waiting for transfers between devices, on_device(): lax.all_to_all(entering, 'head', split_axis=2, concat_axis=1, tiled=True)  24.4 us
    dot_general x5, matrix products, key_value_grads(): jnp.einsum('hqk,qhd->khd', probs.astype(jnp.bfloat16), dout_heads, prefer...  22.1 us
    ppermute x8, waiting for transfers between devices, shifted(): return lax.ppermute(shard, axis, pairs)  21.6 us
    dot_general x5, matrix products, on_device(): jnp.einsum('hqk,khd->qhd', probs.astype(jnp.bfloat16), split_heads(remote...  19.1 us
    reduce_sum x3, other arithmetic, on_device(): row_total = row_total * jnp.exp(row_top - new_top) + jnp.sum(kept, axis=-1)  14.4 us
  transfers between devices with their start and end apart: 9, of which 5 were waited for; matrix products, arithmetic and copies ran while one was open for 15% of the time, Pallas kernels for 0%

commit v1 on v0

v1 whole, which is shorter than its diff:
```python
import jax
import jax.numpy as jnp
from jax import lax
from jax.experimental import pallas as pl
from jax.experimental.pallas import tpu as pltpu
from jax.sharding import PartitionSpec as P

HEAD_DIM = 64
BLOCK = 64
PERSON = 512
HALF = 256
PAIR = 128
LOCAL = 4
WINDOW = 8
SLOTS = 16
QBLOCKS = 32
MESH = pl.DeviceIdType.MESH


def place():
    ctx = lax.axis_index("ctx")
    head = lax.axis_index("head")
    return ctx, head, lax.rem(ctx, 2), lax.rem(lax.div(ctx, 2), 4), lax.div(ctx, 8)


def chain_peers():
    ctx, head, core, z, group = place()
    order = group * 2 + core

    def at(step):
        spot = order + step
        return (lax.div(spot, 2) * 8 + z * 2 + lax.rem(spot, 2), head)

    return at(-1), at(1), order > 0, order < 15


def greet():
    ctx, head, core, z, group = place()
    barrier = pltpu.get_barrier_semaphore()
    for turn in range(1, 16):
        spot = lax.rem(lax.rem(ctx, 8) + 8 * head + turn, 16)
        pl.semaphore_signal(
            barrier, 1, device_id=(group * 8 + lax.rem(spot, 8), lax.div(spot, 8)), device_id_type=MESH
        )
    before, after, has_before, has_after = chain_peers()

    first, last = (core == 0) & has_before, (core == 1) & has_after

    @pl.when(first)
    def _():
        pl.semaphore_signal(barrier, 1, device_id=before, device_id_type=MESH)

    @pl.when(last)
    def _():
        pl.semaphore_signal(barrier, 1, device_id=after, device_id_type=MESH)

    pl.semaphore_wait(barrier, 15 + jnp.where(first | last, 1, 0))


def remote(src, dst, send, recv, device):
    return pltpu.make_async_remote_copy(
        src_ref=src, dst_ref=dst, send_sem=send, recv_sem=recv, device_id=device, device_id_type=MESH
    )


def compact_lists(blocks_ref, counts_ref, lists_ref):
    ctx, head, core, z, group = place()
    first = (group * 2 + core) * QBLOCKS
    slots = blocks_ref[pl.ds(first, QBLOCKS), :] - (first - 2 * (PERSON // BLOCK))
    row = lax.broadcasted_iota(jnp.int32, (QBLOCKS, 512), 0)
    col = lax.broadcasted_iota(jnp.int32, (QBLOCKS, 512), 1)
    spread = jnp.broadcast_to(counts_ref[...], (QBLOCKS, 512))
    counts = jnp.sum(jnp.where(col == row + first, spread, 0), axis=1, keepdims=True)
    lane = lax.broadcasted_iota(jnp.int32, (QBLOCKS, SLOTS), 1)
    out_lane = lax.broadcasted_iota(jnp.int32, (QBLOCKS, 128), 1)
    total = jnp.zeros((QBLOCKS, 1), jnp.int32)
    lists = jnp.broadcast_to(slots[:, 0:1], (QBLOCKS, 128))
    for slot in range(SLOTS):
        value = slots[:, slot : slot + 1]
        seen = jnp.sum(jnp.where((slots == value) & (lane < slot), 1, 0), axis=1, keepdims=True)
        live = jnp.where((seen == 0) & (counts > slot), 1, 0)
        lists = jnp.where((out_lane == total) & (live > 0), value, lists)
        total = total + live
    lists_ref[...] = jnp.where(out_lane == SLOTS, total, lists)


def exchange_in(
    key_ref, value_ref, query_ref, dout_ref, blocks_ref, counts_ref,
    keys_out, values_out, queries_out, douts_out, lists_ref,
    send_sem, recv_sem, halo_send, halo_recv,
):
    ctx, head, core, z, group = place()
    greet()
    owner_core = lax.div(z, 2)
    person = lax.rem(ctx, 4)
    sources = (key_ref, value_ref, query_ref, dout_ref)
    targets = (keys_out, values_out, queries_out, douts_out)
    bases = (2 * PERSON, 2 * PERSON, 0, 0)

    def piece(which, turn):
        to_z = lax.rem(z + turn % 4, 4)
        to_head = lax.rem(head + turn // 4, 2)
        column = pl.multiple_of((to_head * 4 + to_z) * PAIR, PAIR)
        row = pl.multiple_of(bases[which] + person * PERSON + head * HALF, HALF)
        src = sources[which].at[:, pl.ds(column, PAIR)]
        dst = targets[which].at[pl.ds(row, HALF), :]
        return src, dst, (group * 8 + to_z * 2 + owner_core, to_head)

    order = (6, 2, 5, 7, 4, 1, 3, 0)
    for which in range(4):
        for turn in order:
            src, dst, device = piece(which, turn)
            send, recv = send_sem.at[which, turn], recv_sem.at[which, person, head]
            if turn == 0:

                @pl.when(owner_core == core)
                def _():
                    pltpu.make_async_copy(src, dst, recv).start()

                @pl.when(owner_core != core)
                def _():
                    remote(src, dst, send, recv, device).start()
            else:
                remote(src, dst, send, recv, device).start()
    compact_lists(blocks_ref, counts_ref, lists_ref)
    before, after, has_before, has_after = chain_peers()

    def arrive(which, who):
        for half in range(2):
            rows = pl.ds(bases[which] + who * PERSON + half * HALF, HALF)
            part = targets[which].at[rows, :]
            pltpu.make_async_copy(part, part, recv_sem.at[which, who, half]).wait()

    def halo(which, who):
        target = targets[which]
        src = target.at[pl.ds((2 + who) * PERSON, PERSON), :]
        to = 6 + who if who < 2 else who - 2
        dst = target.at[pl.ds(to * PERSON, PERSON), :]
        return remote(
            src, dst, halo_send.at[which, who], halo_recv.at[which, who], before if who < 2 else after
        )

    for which in range(2):
        for who in range(4):
            arrive(which, who)

            @pl.when(has_before if who < 2 else has_after)
            def _():
                halo(which, who).start()

    for which in range(2, 4):
        for who in range(4):
            arrive(which, who)
    for which in range(2):
        for who in range(4):

            @pl.when(has_before if who < 2 else has_after)
            def _():
                halo(which, who).wait_send()

            @pl.when(has_after if who < 2 else has_before)
            def _():
                halo(which, who).wait_recv()

    for which in range(4):
        for turn in order:
            src, dst, device = piece(which, turn)
            copy = remote(src, dst, send_sem.at[which, turn], recv_sem.at[which, person, head], device)
            if turn == 0:

                @pl.when(owner_core != core)
                def _():
                    copy.wait_send()
            else:
                copy.wait_send()


def attend(
    lists_ref, query_ref, dout_ref, key_ref, value_ref, dquery_ref, dkey_ref, dvalue_ref, dkey_sum, dvalue_sum
):
    rows_all = WINDOW * PERSON

    @pl.loop(0, rows_all // PERSON)
    def _(chunk):
        rows = pl.ds(pl.multiple_of(chunk * PERSON, PERSON), PERSON)
        dkey_sum[rows, :] = jnp.zeros((PERSON, PAIR), jnp.float32)
        dvalue_sum[rows, :] = jnp.zeros((PERSON, PAIR), jnp.float32)

    first_head = lax.broadcasted_iota(jnp.int32, (BLOCK, PAIR), 1) < HEAD_DIM
    scale = HEAD_DIM ** (-0.5)

    def both_heads(block):
        nothing = jnp.zeros_like(block)
        return jnp.concatenate(
            [jnp.where(first_head, block, nothing), jnp.where(first_head, nothing, block)], axis=0
        )

    def body(block, live, width):
        q_rows = pl.ds(pl.multiple_of(block * BLOCK, BLOCK), BLOCK)
        spots = [
            pl.ds(pl.multiple_of(lists_ref[block, slot] * BLOCK, BLOCK), BLOCK) for slot in range(width)
        ]
        queries = both_heads(query_ref[q_rows, :])
        douts = both_heads(dout_ref[q_rows, :])
        keys = jnp.concatenate([key_ref[spot, :] for spot in spots], axis=0)
        values = jnp.concatenate([value_ref[spot, :] for spot in spots], axis=0)
        nt = (((1,), (1,)), ((), ()))
        scores = lax.dot_general(keys, queries, nt, preferred_element_type=jnp.float32) * scale
        fixed = (width - 4) * BLOCK
        tail = lax.broadcasted_iota(jnp.int32, (4 * BLOCK, PAIR), 0) + fixed < live * BLOCK
        tail = jnp.where(tail, scores[fixed:], -1e30)
        scores = jnp.concatenate([scores[:fixed], tail], axis=0) if fixed else tail
        top = jnp.max(scores, axis=0, keepdims=True)
        weights = jnp.exp(scores - top)
        probs = weights * (1.0 / jnp.sum(weights, axis=0, keepdims=True))
        probs_b = probs.astype(jnp.bfloat16)
        d_probs = lax.dot_general(values, douts, nt, preferred_element_type=jnp.float32)
        delta = jnp.sum(probs_b.astype(jnp.float32) * d_probs, axis=0, keepdims=True)
        d_scores = (probs * (d_probs - delta)).astype(jnp.bfloat16)
        d_values = jnp.dot(probs_b, douts, preferred_element_type=jnp.float32)
        d_keys = jnp.dot(d_scores, queries, preferred_element_type=jnp.float32)
        d_queries = lax.dot_general(
            d_scores, keys, (((0,), (0,)), ((), ())), preferred_element_type=jnp.float32
        )
        d_queries = jnp.where(first_head, d_queries[:BLOCK], d_queries[BLOCK:]) * scale
        dquery_ref[q_rows, :] = d_queries.astype(jnp.bfloat16)
        for slot, spot in enumerate(spots):
            part = slice(slot * BLOCK, (slot + 1) * BLOCK)
            dvalue_sum[spot, :] += d_values[part]
            dkey_sum[spot, :] += d_keys[part]

    @pl.loop(0, QBLOCKS)
    def _(block):
        live = lists_ref[block, SLOTS]
        for width in (4, 8, 12, 16):

            @pl.when((live <= width) & (live > width - 4))
            def _():
                body(block, live, width)

    @pl.loop(0, rows_all // PERSON)
    def _(chunk):
        rows = pl.ds(pl.multiple_of(chunk * PERSON, PERSON), PERSON)
        dkey_ref[rows, :] = (dkey_sum[rows, :] * scale).astype(jnp.bfloat16)
        dvalue_ref[rows, :] = dvalue_sum[rows, :].astype(jnp.bfloat16)


def exchange_out(
    dquery_ref, dkey_ref, dvalue_ref,
    dquery_out, dkey_out, dvalue_out,
    arrived, total, send_sem, recv_sem, halo_send, halo_recv,
):
    ctx, head, core, z, group = place()
    greet()
    before, after, has_before, has_after = chain_peers()
    parts = (dkey_ref, dvalue_ref)
    outs = (dquery_out, dkey_out, dvalue_out)

    def halo(which, who):
        spot = 6 + who if who < 2 else who - 2
        return remote(
            parts[which].at[pl.ds(spot * PERSON, PERSON), :],
            arrived.at[which, who],
            halo_send.at[which, who],
            halo_recv.at[which, who],
            after if who < 2 else before,
        )

    for which in range(2):
        for who in range(4):

            @pl.when(has_after if who < 2 else has_before)
            def _():
                halo(which, who).start()

    column = pl.multiple_of((head * 4 + z) * PAIR, PAIR)

    def piece(which, who, half):
        src = dquery_ref if which == 0 else total.at[which - 1]
        src = src.at[pl.ds(who * PERSON + half * HALF, HALF), :]
        dst = outs[which].at[:, pl.ds(column, PAIR)]
        device = (group * 8 + core * 4 + who, jnp.int32(half))
        return src, dst, device

    pair = head * 4 + z

    def send(which, who, half):
        src, dst, device = piece(which, who, half)
        recv = recv_sem.at[which, pair]
        itself = (device[0] == ctx) & (head == half)

        @pl.when(itself)
        def _():
            pltpu.make_async_copy(src, dst, recv).start()

        @pl.when(jnp.logical_not(itself))
        def _():
            remote(src, dst, send_sem.at[which, who, half], recv, device).start()

    for who in range(4):
        for half in range(2):
            send(0, who, half)
    for which in range(2):
        for who in range(4):
            own = parts[which][pl.ds((2 + who) * PERSON, PERSON), :].astype(jnp.float32)
            rows = pl.ds(who * PERSON, PERSON)
            there = has_before if who < 2 else has_after

            @pl.when(there)
            def _():
                halo(which, who).wait_recv()
                total[which, rows, :] = (own + arrived[which, who].astype(jnp.float32)).astype(jnp.bfloat16)

            @pl.when(jnp.logical_not(there))
            def _():
                total[which, rows, :] = own.astype(jnp.bfloat16)

            for half in range(2):
                send(which + 1, who, half)

    for which in range(2):
        for who in range(4):

            @pl.when(has_after if who < 2 else has_before)
            def _():
                halo(which, who).wait_send()

    for which in range(3):
        for who in range(4):
            for half in range(2):
                src, dst, device = piece(which, who, half)
                itself = (device[0] == ctx) & (head == half)

                @pl.when(jnp.logical_not(itself))
                def _():
                    remote(
                        src, dst, send_sem.at[which, who, half], recv_sem.at[which, pair], device
                    ).wait_send()

        for source in range(8):
            part = outs[which].at[:, pl.ds(source * PAIR, PAIR)]
            pltpu.make_async_copy(part, part, recv_sem.at[which, source]).wait()


def on_device(queries, keys_in, values, d_out, pair_blocks, pair_count):
    anywhere = pl.BlockSpec(memory_space=pl.ANY)
    vmem = pl.BlockSpec(memory_space=pltpu.VMEM)
    dma = pltpu.SemaphoreType.DMA
    wide = jax.ShapeDtypeStruct((WINDOW * PERSON, PAIR), jnp.bfloat16)
    narrow = jax.ShapeDtypeStruct((LOCAL * PERSON, PAIR), jnp.bfloat16)
    rows = jax.ShapeDtypeStruct(queries.shape, jnp.bfloat16)
    keys, vals, query, dout, lists = pl.pallas_call(
        exchange_in,
        out_shape=(wide, wide, narrow, narrow, jax.ShapeDtypeStruct((QBLOCKS, 128), jnp.int32)),
        in_specs=[anywhere] * 4 + [vmem] * 2,
        out_specs=(anywhere,) * 4 + (vmem,),
        scratch_shapes=[dma((4, 8)), dma((4, 4, 2)), dma((2, 4)), dma((2, 4))],
        compiler_params=pltpu.CompilerParams(collective_id=0, has_side_effects=True),
        name="exchange_in",
    )(keys_in, values, queries, d_out, pair_blocks, pair_count.reshape(1, -1))
    d_query, d_key, d_value = pl.pallas_call(
        attend,
        out_shape=(narrow, wide, wide),
        in_specs=[pl.BlockSpec(memory_space=pltpu.SMEM)] + [vmem] * 4,
        out_specs=(vmem,) * 3,
        scratch_shapes=[pltpu.VMEM((WINDOW * PERSON, PAIR), jnp.float32)] * 2,
        compiler_params=pltpu.CompilerParams(vmem_limit_bytes=40 << 20),
        name="attend",
    )(lists, query, dout, keys, vals)
    return pl.pallas_call(
        exchange_out,
        out_shape=(rows,) * 3,
        in_specs=[anywhere, vmem, vmem],
        out_specs=(anywhere,) * 3,
        scratch_shapes=[
            pltpu.VMEM((2, 4, PERSON, PAIR), jnp.bfloat16),
            pltpu.VMEM((2, LOCAL * PERSON, PAIR), jnp.bfloat16),
            dma((3, 4, 2)), dma((3, 8)), dma((2, 4)), dma((2, 4)),
        ],
        compiler_params=pltpu.CompilerParams(collective_id=1, has_side_effects=True),
        name="exchange_out",
    )(d_query, d_key, d_value)


def solution(mesh):
    tokens = P(("ctx", "head"), None)
    return jax.shard_map(
        on_device,
        mesh=mesh,
        in_specs=(tokens,) * 4 + (P(), P()),
        out_specs=(tokens,) * 3,
        check_vma=False,
    )
```

time: 282 us -> 112 us (0.40)
  the two profiles are of different devices: /device:TPU:121 before, /device:TPU:3 now
where the time goes in v1:
time: 112 us; the launch traced here: 111 us
  Pallas kernels  97 us (87%)
  local copies, waits for them, and re-layouts  13.5 us (12%)
    pallas_call x1, Pallas kernels, on_device(): pl.pallas_call(exchange_out, out_shape=(rows,) * 3, in_specs=[anywhere, v...  41.6 us
    pallas_call x1, Pallas kernels, on_device(): pl.pallas_call(exchange_in, out_shape=(wide, wide, narrow, narrow, jax.Sh...  32.6 us
    pallas_call x1, Pallas kernels, on_device(): pl.pallas_call(attend, out_shape=(narrow, wide, wide), in_specs=[pl.Block...  22.8 us
    unnamed x24, local copies, waits for them, and re-layouts  13.5 us

profile of v1, /device:TPU:3, one launch (start us, length us, event | category | flops | bytes accessed | tf_op | source)
XLA Modules:
  0.0 111.2 jit_solution(14051739192593299627)
XLA Ops:
  0.6 1.6 %copy.9.blocks_ref = s32[512,16]{1,0:T(8,128)} copy(s32[512,16]{0,1:T(8,128)} %param.10) | data formatting | bytes 65536 | tf_op args[4]
  2.2 32.6 %exchange_in.1 = (bf16[4096,128]{1,0:T(8,128)(2,1)}, bf16[4096,128]{1,0:T(8,128)(2,1)}, bf16[2048,128]{1,0:T(8,128)(2,1)}, bf16[2048,128]{1,0:T(8,128)(2,1)}, s32[32,128]{1,0:T(8,128)}) custom-call(bf16[256,1024]{1,0:T(8,128)(2,1)} %key_ref.1, bf16[256,1024]{1,0:T(8,128)(2,1)} %value_ref.1, bf16[256,1024]{1,0:T(8,128)(2,1)} %query_ref.1, ...), custom_call_target="tpu_custom_call" | custom-call | tf_op jit(solution)/shard_map/exchange_in/pallas_call | solution.py:352
  34.8 0.0 copy-start
  34.8 1.2 %copy-done = bf16[4096,128]{1,0:T(8,128)(2,1)S(1)} copy-done((bf16[4096,128]{1,0:T(8,128)(2,1)S(1)}, bf16[4096,128]{1,0:T(8,128)(2,1)}, u32[]{:S(2)}) %copy-start) | copy-done | bytes 1048600
  36.0 0.0 copy-start.1
  36.0 1.2 %copy-done.1 = bf16[4096,128]{1,0:T(8,128)(2,1)S(1)} copy-done((bf16[4096,128]{1,0:T(8,128)(2,1)S(1)}, bf16[4096,128]{1,0:T(8,128)(2,1)}, u32[]{:S(2)}) %copy-start.1) | copy-done | bytes 1048600
  37.3 0.0 copy-start.5
  37.3 1.0 copy-done.5
  38.3 0.0 copy-start.6
  38.3 1.0 copy-done.6
  39.3 0.0 copy-start.7
  39.4 0.7 copy-done.7
  40.1 22.8 %attend.1 = (bf16[2048,128]{1,0:T(8,128)(2,1)S(1)}, bf16[4096,128]{1,0:T(8,128)(2,1)S(1)}, bf16[4096,128]{1,0:T(8,128)(2,1)S(1)}) custom-call(s32[32,128]{1,0:T(8,128)S(1)} %copy-done.7, bf16[2048,128]{1,0:T(8,128)(2,1)S(1)} %copy-done.5, bf16[2048,128]{1,0:T(8,128)(2,1)S(1)} %copy-done.6, bf16[4096,128]{1,0:T(8,128)(2,1)S(1)} %copy-done, ...), custom_call_target="tpu_custom_call" | custom-call | tf_op jit(solution)/shard_map/attend/pallas_call | solution.py:361
  62.9 0.0 copy-start.2
  62.9 1.0 copy-done.2
  63.8 0.0 copy-start.3
  63.8 1.0 copy-done.3
  64.8 0.0 copy-start.4
  64.8 0.8 copy-done.4
  65.6 41.6 %exchange_out.1 = (bf16[256,1024]{1,0:T(8,128)(2,1)}, bf16[256,1024]{1,0:T(8,128)(2,1)}, bf16[256,1024]{1,0:T(8,128)(2,1)}) custom-call(bf16[2048,128]{1,0:T(8,128)(2,1)} %copy-done.4, bf16[4096,128]{1,0:T(8,128)(2,1)} %copy-done.2, bf16[4096,128]{1,0:T(8,128)(2,1)} %copy-done.3), custom_call_target="tpu_custom_call" | custom-call | tf_op jit(solution)/shard_map/exchange_out/pallas_call | solution.py:370
  107.2 0.0 copy-start.9
  107.2 1.9 %copy.13 = bf16[256,1024]{1,0:T(8,128)(2,1)} copy(bf16[256,1024]{1,0:T(8,128)(2,1)} %get-tuple-element.22) | data formatting | bytes 1048576
  109.2 0.0 copy-done.9
  109.2 0.0 copy-start.8
  109.2 0.8 copy.14
  110.0 0.4 copy-done.8
  110.4 0.8 copy.15
Async XLA Ops:
  34.8 1.2 %copy-start = (bf16[4096,128]{1,0:T(8,128)(2,1)S(1)}, bf16[4096,128]{1,0:T(8,128)(2,1)}, u32[]{:S(2)}) copy-start(bf16[4096,128]{1,0:T(8,128)(2,1)} %get-tuple-element.14.key_ref) | copy-start | bytes 3145732
  36.0 1.2 %copy-start.1 = (bf16[4096,128]{1,0:T(8,128)(2,1)S(1)}, bf16[4096,128]{1,0:T(8,128)(2,1)}, u32[]{:S(2)}) copy-start(bf16[4096,128]{1,0:T(8,128)(2,1)} %get-tuple-element.15.value_ref) | copy-start | bytes 3145732
  37.3 1.0 copy-start.5
  38.3 1.0 copy-start.6
  39.3 0.7 copy-start.7
  62.9 1.0 copy-start.2
  63.8 1.0 copy-start.3
  64.8 0.8 copy-start.4
  107.2 1.9 %copy-start.9 = (bf16[256,1024]{1,0:T(8,128)(2,1)S(1)}, bf16[256,1024]{1,0:T(8,128)(2,1)}, u32[]{:S(2)}) copy-start(bf16[256,1024]{1,0:T(8,128)(2,1)} %get-tuple-element.23) | copy-start | bytes 1572868
  109.2 1.2 %copy-start.8 = (bf16[256,1024]{1,0:T(8,128)(2,1)S(1)}, bf16[256,1024]{1,0:T(8,128)(2,1)}, u32[]{:S(2)}) copy-start(bf16[256,1024]{1,0:T(8,128)(2,1)} %get-tuple-element.24) | copy-start | bytes 1572868

commit v2 on v1

--- a/solution.py
+++ b/solution.py
@@ -14,6 +14,9 @@
 WINDOW = 8
 SLOTS = 16
 QBLOCKS = 32
+LIST_ROWS = 24
+STEP = 4
+GROUP = 2
 MESH = pl.DeviceIdType.MESH
 
 
@@ -66,30 +69,43 @@
 def compact_lists(blocks_ref, counts_ref, lists_ref):
     ctx, head, core, z, group = place()
     first = (group * 2 + core) * QBLOCKS
-    slots = blocks_ref[pl.ds(first, QBLOCKS), :] - (first - 2 * (PERSON // BLOCK))
-    row = lax.broadcasted_iota(jnp.int32, (QBLOCKS, 512), 0)
-    col = lax.broadcasted_iota(jnp.int32, (QBLOCKS, 512), 1)
-    spread = jnp.broadcast_to(counts_ref[...], (QBLOCKS, 512))
-    counts = jnp.sum(jnp.where(col == row + first, spread, 0), axis=1, keepdims=True)
-    lane = lax.broadcasted_iota(jnp.int32, (QBLOCKS, SLOTS), 1)
-    out_lane = lax.broadcasted_iota(jnp.int32, (QBLOCKS, 128), 1)
-    total = jnp.zeros((QBLOCKS, 1), jnp.int32)
-    lists = jnp.broadcast_to(slots[:, 0:1], (QBLOCKS, 128))
+    row = lax.broadcasted_iota(jnp.int32, (SLOTS, 512), 0)
+    slots = blocks_ref[...] - (first - 2 * (PERSON // BLOCK))
+    counts = counts_ref[...]
+    out_row = lax.broadcasted_iota(jnp.int32, (LIST_ROWS, 512), 0)
+    total = jnp.zeros((1, 512), jnp.int32)
+    lists = jnp.broadcast_to(slots[0:1], (LIST_ROWS, 512))
     for slot in range(SLOTS):
-        value = slots[:, slot : slot + 1]
-        seen = jnp.sum(jnp.where((slots == value) & (lane < slot), 1, 0), axis=1, keepdims=True)
+        value = slots[slot : slot + 1]
+        seen = jnp.sum(jnp.where((slots == value) & (row < slot), 1, 0), axis=0, keepdims=True)
         live = jnp.where((seen == 0) & (counts > slot), 1, 0)
-        lists = jnp.where((out_lane == total) & (live > 0), value, lists)
+        lists = jnp.where((out_row == total) & (live > 0), value, lists)
         total = total + live
-    lists_ref[...] = jnp.where(out_lane == SLOTS, total, lists)
+    lists = jnp.where(out_row == SLOTS, total, lists)
+    lists = pltpu.roll(lists, lax.rem(512 - first, 512), 1)[:, :128]
+    across = lax.broadcasted_iota(jnp.int32, (128, 128), 1)
+    down = lax.broadcasted_iota(jnp.int32, (128, 128), 0)
+    size = jnp.where(across[0:1] < QBLOCKS, lists[SLOTS : SLOTS + 1], -1)
+    size = jnp.broadcast_to(size, (128, 128))
+    own = jnp.sum(jnp.where(across == down, size, 0), axis=1, keepdims=True)
+    ahead = jnp.where((size > own) | ((size == own) & (across < down)), 1, 0)
+    rank = jnp.sum(ahead, axis=1, keepdims=True)
+    ranked = jnp.sum(jnp.where(rank == across, down, 0), axis=0, keepdims=True)
+    lists_ref[...] = jnp.where(out_row[:, :128] == SLOTS + 1, ranked, lists)
 
 
 def exchange_in(
     key_ref, value_ref, query_ref, dout_ref, blocks_ref, counts_ref,
     keys_out, values_out, queries_out, douts_out, lists_ref,
-    send_sem, recv_sem, halo_send, halo_recv,
+    blocks_vmem, counts_vmem, table_sem, send_sem, recv_sem, halo_send, halo_recv,
 ):
     ctx, head, core, z, group = place()
+    tables = [
+        pltpu.make_async_copy(blocks_ref, blocks_vmem, table_sem.at[0]),
+        pltpu.make_async_copy(counts_ref, counts_vmem, table_sem.at[1]),
+    ]
+    for table in tables:
+        table.start()
     greet()
     owner_core = lax.div(z, 2)
     person = lax.rem(ctx, 4)
@@ -122,7 +138,9 @@
                     remote(src, dst, send, recv, device).start()
             else:
                 remote(src, dst, send, recv, device).start()
-    compact_lists(blocks_ref, counts_ref, lists_ref)
+    for table in tables:
+        table.wait()
+    compact_lists(blocks_vmem, counts_vmem, lists_ref)
     before, after, has_before, has_after = chain_peers()
 
     def arrive(which, who):
@@ -188,60 +206,90 @@
 
     first_head = lax.broadcasted_iota(jnp.int32, (BLOCK, PAIR), 1) < HEAD_DIM
     scale = HEAD_DIM ** (-0.5)
+    nt = (((1,), (1,)), ((), ()))
+    tn = (((0,), (0,)), ((), ()))
 
     def both_heads(block):
         nothing = jnp.zeros_like(block)
+        return [jnp.where(first_head, block, nothing), jnp.where(first_head, nothing, block)]
+
+    def spread(one, two):
+        upper = jnp.concatenate(both_heads(one), axis=0)
+        lower = jnp.concatenate(both_heads(two), axis=0)
+        nothing = jnp.zeros_like(upper)
         return jnp.concatenate(
-            [jnp.where(first_head, block, nothing), jnp.where(first_head, nothing, block)], axis=0
+            [jnp.concatenate([upper, nothing], axis=1), jnp.concatenate([nothing, lower], axis=1)], axis=0
         )
 
-    def body(block, live, width):
-        q_rows = pl.ds(pl.multiple_of(block * BLOCK, BLOCK), BLOCK)
+    def load(pair, width):
+        blocks = [lists_ref[SLOTS + 1, pair * 2 + i] for i in range(2)]
+        lives = [lists_ref[SLOTS, block] for block in blocks]
+        q_rows = [pl.ds(pl.multiple_of(block * BLOCK, BLOCK), BLOCK) for block in blocks]
         spots = [
-            pl.ds(pl.multiple_of(lists_ref[block, slot] * BLOCK, BLOCK), BLOCK) for slot in range(width)
+            [pl.ds(pl.multiple_of(lists_ref[slot, block] * BLOCK, BLOCK), BLOCK) for slot in range(width)]
+            for block in blocks
         ]
-        queries = both_heads(query_ref[q_rows, :])
-        douts = both_heads(dout_ref[q_rows, :])
-        keys = jnp.concatenate([key_ref[spot, :] for spot in spots], axis=0)
-        values = jnp.concatenate([value_ref[spot, :] for spot in spots], axis=0)
-        nt = (((1,), (1,)), ((), ()))
-        scores = lax.dot_general(keys, queries, nt, preferred_element_type=jnp.float32) * scale
-        fixed = (width - 4) * BLOCK
-        tail = lax.broadcasted_iota(jnp.int32, (4 * BLOCK, PAIR), 0) + fixed < live * BLOCK
-        tail = jnp.where(tail, scores[fixed:], -1e30)
-        scores = jnp.concatenate([scores[:fixed], tail], axis=0) if fixed else tail
+        return lives, q_rows, spots
+
+    def softmax(width, lives, q_rows, spots):
+        queries = spread(*[(query_ref[rows, :] * scale).astype(jnp.bfloat16) for rows in q_rows])
+        douts = spread(*[dout_ref[rows, :] for rows in q_rows])
+        keys = [jnp.concatenate([key_ref[spot, :] for spot in some], axis=0) for some in spots]
+        values = [jnp.concatenate([value_ref[spot, :] for spot in some], axis=0) for some in spots]
+        both_keys = jnp.concatenate(keys, axis=1)
+        both_values = jnp.concatenate(values, axis=1)
+        scores = lax.dot_general(both_keys, queries, nt, preferred_element_type=jnp.float32)
+        lane = lax.broadcasted_iota(jnp.int32, (1, 2 * PAIR), 1)
+        live = jnp.where(lane < PAIR, lives[0], lives[1])
+        scores = jnp.concatenate(
+            [
+                jnp.where(live > slot, scores[slot * BLOCK : (slot + 1) * BLOCK], -1e30)
+                for slot in range(width)
+            ],
+            axis=0,
+        )
         top = jnp.max(scores, axis=0, keepdims=True)
         weights = jnp.exp(scores - top)
-        probs = weights * (1.0 / jnp.sum(weights, axis=0, keepdims=True))
+        d_probs = lax.dot_general(both_values, douts, nt, preferred_element_type=jnp.float32)
+        share = 1.0 / jnp.sum(weights, axis=0, keepdims=True)
+        delta = jnp.sum(weights * d_probs, axis=0, keepdims=True) * share
+        probs = weights * share
         probs_b = probs.astype(jnp.bfloat16)
-        d_probs = lax.dot_general(values, douts, nt, preferred_element_type=jnp.float32)
-        delta = jnp.sum(probs_b.astype(jnp.float32) * d_probs, axis=0, keepdims=True)
         d_scores = (probs * (d_probs - delta)).astype(jnp.bfloat16)
+        return queries, douts, keys, probs_b, d_scores
+
+    def gradients(q_rows, spots, queries, douts, keys, probs_b, d_scores):
         d_values = jnp.dot(probs_b, douts, preferred_element_type=jnp.float32)
         d_keys = jnp.dot(d_scores, queries, preferred_element_type=jnp.float32)
-        d_queries = lax.dot_general(
-            d_scores, keys, (((0,), (0,)), ((), ())), preferred_element_type=jnp.float32
-        )
-        d_queries = jnp.where(first_head, d_queries[:BLOCK], d_queries[BLOCK:]) * scale
-        dquery_ref[q_rows, :] = d_queries.astype(jnp.bfloat16)
-        for slot, spot in enumerate(spots):
-            part = slice(slot * BLOCK, (slot + 1) * BLOCK)
-            dvalue_sum[spot, :] += d_values[part]
-            dkey_sum[spot, :] += d_keys[part]
-
-    @pl.loop(0, QBLOCKS)
-    def _(block):
-        live = lists_ref[block, SLOTS]
-        for width in (4, 8, 12, 16):
-
-            @pl.when((live <= width) & (live > width - 4))
-            def _():
-                body(block, live, width)
+        for i in range(2):
+            lanes = slice(i * PAIR, (i + 1) * PAIR)
+            d_queries = lax.dot_general(d_scores[:, lanes], keys[i], tn, preferred_element_type=jnp.float32)
+            d_queries = jnp.where(first_head, d_queries[:BLOCK], d_queries[BLOCK:]) * scale
+            dquery_ref[q_rows[i], :] = d_queries.astype(jnp.bfloat16)
+            for slot, spot in enumerate(spots[i]):
+                part = slice(slot * BLOCK, (slot + 1) * BLOCK)
+                dvalue_sum[spot, :] += d_values[part, lanes]
+                dkey_sum[spot, :] += d_keys[part, lanes]
+
+    def body(group, width):
+        loaded = [load(group * GROUP + i, width) for i in range(GROUP)]
+        done = [softmax(width, *some) for some in loaded]
+        for some, values in zip(loaded, done):
+            gradients(*some[1:], *values)
+
+    @pl.loop(0, QBLOCKS // (2 * GROUP))
+    def _(group):
+        live = lists_ref[SLOTS, lists_ref[SLOTS + 1, group * 2 * GROUP]]
+        for width in range(STEP, SLOTS + 1, STEP):
+
+            @pl.when((live <= width) & (live > width - STEP))
+            def _():
+                body(group, width)
 
     @pl.loop(0, rows_all // PERSON)
     def _(chunk):
         rows = pl.ds(pl.multiple_of(chunk * PERSON, PERSON), PERSON)
-        dkey_ref[rows, :] = (dkey_sum[rows, :] * scale).astype(jnp.bfloat16)
+        dkey_ref[rows, :] = dkey_sum[rows, :].astype(jnp.bfloat16)
         dvalue_ref[rows, :] = dvalue_sum[rows, :].astype(jnp.bfloat16)
 
 
@@ -342,44 +390,71 @@
             pltpu.make_async_copy(part, part, recv_sem.at[which, source]).wait()
 
 
+def put_out(dquery_ref, dkey_ref, dvalue_ref, dquery_out, dkey_out, dvalue_out, sem):
+    pairs = ((dquery_ref, dquery_out), (dkey_ref, dkey_out), (dvalue_ref, dvalue_out))
+    copies = [pltpu.make_async_copy(src, dst, sem.at[i]) for i, (src, dst) in enumerate(pairs)]
+    for copy in copies:
+        copy.start()
+    for copy in copies:
+        copy.wait()
+
+
 def on_device(queries, keys_in, values, d_out, pair_blocks, pair_count):
-    anywhere = pl.BlockSpec(memory_space=pl.ANY)
+    hbm = pl.BlockSpec(memory_space=pltpu.HBM)
     vmem = pl.BlockSpec(memory_space=pltpu.VMEM)
     dma = pltpu.SemaphoreType.DMA
     wide = jax.ShapeDtypeStruct((WINDOW * PERSON, PAIR), jnp.bfloat16)
     narrow = jax.ShapeDtypeStruct((LOCAL * PERSON, PAIR), jnp.bfloat16)
     rows = jax.ShapeDtypeStruct(queries.shape, jnp.bfloat16)
+    blocks = pair_count.shape[0]
+    tables = (pair_blocks.T, pair_count.reshape(1, blocks))
+    sources = [
+        pltpu.with_memory_space_constraint(x, pltpu.HBM) for x in (keys_in, values, queries, d_out) + tables
+    ]
     keys, vals, query, dout, lists = pl.pallas_call(
         exchange_in,
-        out_shape=(wide, wide, narrow, narrow, jax.ShapeDtypeStruct((QBLOCKS, 128), jnp.int32)),
-        in_specs=[anywhere] * 4 + [vmem] * 2,
-        out_specs=(anywhere,) * 4 + (vmem,),
-        scratch_shapes=[dma((4, 8)), dma((4, 4, 2)), dma((2, 4)), dma((2, 4))],
-        compiler_params=pltpu.CompilerParams(collective_id=0, has_side_effects=True),
+        out_shape=(wide, wide, narrow, narrow, jax.ShapeDtypeStruct((LIST_ROWS, 128), jnp.int32)),
+        in_specs=[hbm] * 6,
+        out_specs=(vmem,) * 5,
+        scratch_shapes=[
+            pltpu.VMEM((SLOTS, blocks), jnp.int32),
+            pltpu.VMEM((1, blocks), jnp.int32),
+            dma((2,)), dma((4, 8)), dma((4, 4, 2)), dma((2, 4)), dma((2, 4)),
+        ],
+        compiler_params=pltpu.CompilerParams(collective_id=0, has_side_effects=True, vmem_limit_bytes=16 << 20),
         name="exchange_in",
-    )(keys_in, values, queries, d_out, pair_blocks, pair_count.reshape(1, -1))
+    )(*sources)
     d_query, d_key, d_value = pl.pallas_call(
         attend,
         out_shape=(narrow, wide, wide),
         in_specs=[pl.BlockSpec(memory_space=pltpu.SMEM)] + [vmem] * 4,
         out_specs=(vmem,) * 3,
         scratch_shapes=[pltpu.VMEM((WINDOW * PERSON, PAIR), jnp.float32)] * 2,
-        compiler_params=pltpu.CompilerParams(vmem_limit_bytes=40 << 20),
+        compiler_params=pltpu.CompilerParams(vmem_limit_bytes=24 << 20),
         name="attend",
     )(lists, query, dout, keys, vals)
-    return pl.pallas_call(
+    results = pl.pallas_call(
         exchange_out,
         out_shape=(rows,) * 3,
-        in_specs=[anywhere, vmem, vmem],
-        out_specs=(anywhere,) * 3,
+        in_specs=[vmem] * 3,
+        out_specs=(vmem,) * 3,
         scratch_shapes=[
             pltpu.VMEM((2, 4, PERSON, PAIR), jnp.bfloat16),
             pltpu.VMEM((2, LOCAL * PERSON, PAIR), jnp.bfloat16),
             dma((3, 4, 2)), dma((3, 8)), dma((2, 4)), dma((2, 4)),
         ],
-        compiler_params=pltpu.CompilerParams(collective_id=1, has_side_effects=True),
+        compiler_params=pltpu.CompilerParams(collective_id=1, has_side_effects=True, vmem_limit_bytes=16 << 20),
         name="exchange_out",
     )(d_query, d_key, d_value)
+    return pl.pallas_call(
+        put_out,
+        out_shape=(rows,) * 3,
+        in_specs=[vmem] * 3,
+        out_specs=(hbm,) * 3,
+        scratch_shapes=[dma((3,))],
+        compiler_params=pltpu.CompilerParams(vmem_limit_bytes=8 << 20),
+        name="put_out",
+    )(*results)
 
 
 def solution(mesh):

time: 112 us -> 80.8 us (0.72)
  Pallas kernels: 97 us -> 80 us
  local copies, waits for them, and re-layouts: 13.5 us -> 0 us
    unnamed x24 -> x0, local copies, waits for them, and re-layouts: 13.5 us -> none
    pallas_call x1, Pallas kernels: 22.8 us -> 15 us  [on_device(): pl.pallas_call(attend, out_shape=(narrow, wide, wide), in_specs=[pl.Block...]
    pallas_call x1 -> x2, Pallas kernels: 41.6 us -> 33.8 us  [the longest x1 32.7 us: on_device(): pl.pallas_call(exchange_out, out_shape=(rows,) * 3, in_specs=[vmem] * 3,...]
    pallas_call x1, Pallas kernels: 32.6 us -> 31.2 us  [on_device(): pl.pallas_call(exchange_in, out_shape=(wide, wide, narrow, narrow, jax.Sh...]
where the time goes in v2:
time: 80.8 us; the launch traced here: 80.6 us
  Pallas kernels  80 us (99%)
    pallas_call x1, Pallas kernels, on_device(): pl.pallas_call(exchange_out, out_shape=(rows,) * 3, in_specs=[vmem] * 3,...  32.7 us
    pallas_call x1, Pallas kernels, on_device(): pl.pallas_call(exchange_in, out_shape=(wide, wide, narrow, narrow, jax.Sh...  31.2 us
    pallas_call x1, Pallas kernels, on_device(): pl.pallas_call(attend, out_shape=(narrow, wide, wide), in_specs=[pl.Block...  15 us

profile of v2, /device:TPU:3, one launch (start us, length us, event | category | flops | bytes accessed | tf_op | source)
XLA Modules:
  0.0 80.6 jit_solution(1400366030020601653)
XLA Ops:
  0.6 31.2 %exchange_in.1 = (bf16[4096,128]{1,0:T(8,128)(2,1)S(1)}, bf16[4096,128]{1,0:T(8,128)(2,1)S(1)}, bf16[2048,128]{1,0:T(8,128)(2,1)S(1)}, bf16[2048,128]{1,0:T(8,128)(2,1)S(1)}, s32[24,128]{1,0:T(8,128)S(1)}) custom-call(bf16[256,1024]{1,0:T(8,128)(2,1)} %key_ref.1, bf16[256,1024]{1,0:T(8,128)(2,1)} %value_ref.1, bf16[256,1024]{1,0:T(8,128)(2,1)} %query_ref.1, ...), custom_call_target="tpu_custom_call" | custom-call | tf_op jit(solution)/shard_map/exchange_in/pallas_call | solution.py:414
  31.8 15.0 %attend.1 = (bf16[2048,128]{1,0:T(8,128)(2,1)S(1)}, bf16[4096,128]{1,0:T(8,128)(2,1)S(1)}, bf16[4096,128]{1,0:T(8,128)(2,1)S(1)}) custom-call(s32[24,128]{1,0:T(8,128)S(1)} %get-tuple-element.14.lists_ref, bf16[2048,128]{1,0:T(8,128)(2,1)S(1)} %get-tuple-element.15.query_ref, bf16[2048,128]{1,0:T(8,128)(2,1)S(1)} %get-tuple-element.16.dout_ref, ...), custom_call_target="tpu_custom_call" | custom-call | tf_op jit(solution)/shard_map/attend/pallas_call | solution.py:427
  46.8 32.7 %exchange_out.1 = (bf16[256,1024]{1,0:T(8,128)(2,1)S(1)}, bf16[256,1024]{1,0:T(8,128)(2,1)S(1)}, bf16[256,1024]{1,0:T(8,128)(2,1)S(1)}) custom-call(bf16[2048,128]{1,0:T(8,128)(2,1)S(1)} %get-tuple-element.19.dquery_ref, bf16[4096,128]{1,0:T(8,128)(2,1)S(1)} %get-tuple-element.20.dkey_ref, bf16[4096,128]{1,0:T(8,128)(2,1)S(1)} %get-tuple-element.21.dvalue_ref), custom_call_target="tpu_custom_call" | custom-call | tf_op jit(solution)/shard_map/exchange_out/pallas_call | solution.py:436
  79.4 1.2 %put_out.1 = (bf16[256,1024]{1,0:T(8,128)(2,1)}, bf16[256,1024]{1,0:T(8,128)(2,1)}, bf16[256,1024]{1,0:T(8,128)(2,1)}) custom-call(bf16[256,1024]{1,0:T(8,128)(2,1)S(1)} %get-tuple-element.22.dquery_ref, bf16[256,1024]{1,0:T(8,128)(2,1)S(1)} %get-tuple-element.23.dkey_ref, bf16[256,1024]{1,0:T(8,128)(2,1)S(1)} %get-tuple-element.24.dvalue_ref), custom_call_target="tpu_custom_call" | custom-call | tf_op jit(solution)/shard_map/put_out/pallas_call | solution.py:449

commit v3 on v2

--- a/solution.py
+++ b/solution.py
@@ -16,6 +16,7 @@
 QBLOCKS = 32
 LIST_ROWS = 24
 STEP = 4
+GROUPS = 8
 GROUP = 2
 MESH = pl.DeviceIdType.MESH
 
@@ -26,38 +27,124 @@
     return ctx, head, lax.rem(ctx, 2), lax.rem(lax.div(ctx, 2), 4), lax.div(ctx, 8)
 
 
-def chain_peers():
-    ctx, head, core, z, group = place()
-    order = group * 2 + core
-
-    def at(step):
-        spot = order + step
-        return (lax.div(spot, 2) * 8 + z * 2 + lax.rem(spot, 2), head)
-
-    return at(-1), at(1), order > 0, order < 15
+def neighbours():
+    ctx, head, core, z, group = place()
+    far_group = group - 1 + 2 * core
+    near = (ctx + 1 - 2 * core, head)
+    far = (far_group * 8 + z * 2 + 1 - core, head)
+    return near, far, (far_group >= 0) & (far_group < GROUPS), 2 - 2 * core, 2 * core
+
+
+def on_edge(edge_core):
+    ctx, head, core, z, group = place()
+    return (core == edge_core) & (group == GROUPS // 2 - edge_core)
+
+
+def relays(edge_core):
+    ctx, head, core, z, group = place()
+    return [
+        ((k * edge_core + (GROUPS - 1 - k) * (1 - edge_core)) * 8 + z * 2 + 1 - edge_core, head) for k in range(3)
+    ]
+
+
+def relay_role():
+    ctx, head, core, z, group = place()
+    turn = group * (1 - core) + (GROUPS - 1 - group) * core
+    target = ((GROUPS // 2 - core) * 8 + z * 2 + core, head)
+    other = ((GROUPS // 2 - 1 + core) * 8 + z * 2 + 1 - core, head)
+    return turn < 3, turn + 1, target, other
 
 
 def greet():
     ctx, head, core, z, group = place()
     barrier = pltpu.get_barrier_semaphore()
+
+    def hello(device):
+        pl.semaphore_signal(barrier, 1, device_id=device, device_id_type=MESH)
+
     for turn in range(1, 16):
         spot = lax.rem(lax.rem(ctx, 8) + 8 * head + turn, 16)
-        pl.semaphore_signal(
-            barrier, 1, device_id=(group * 8 + lax.rem(spot, 8), lax.div(spot, 8)), device_id_type=MESH
+        hello((group * 8 + lax.rem(spot, 8), lax.div(spot, 8)))
+    near, far, has_far, near_first, far_first = neighbours()
+    edge = on_edge(0) | on_edge(1)
+    is_relay, turn, target, other = relay_role()
+
+    @pl.when(has_far)
+    def _():
+        hello(far)
+
+    @pl.when(is_relay)
+    def _():
+        hello(other)
+
+    count = 15 + jnp.where(has_far, 1, 0) + jnp.where(edge, 3, 0)
+    pl.semaphore_wait(barrier, count)
+
+
+def far_pieces(source_of, target_of, relay_buf, far_send, far_recv, relay_send, relay_recv):
+    ctx, head, core, z, group = place()
+    near, far, has_far, near_first, far_first = neighbours()
+    edge = on_edge(0) | on_edge(1)
+    is_relay, turn, target, other = relay_role()
+
+    def direct(which, q):
+        return remote(
+            source_of(which, q), target_of(which, q, 1 - core), far_send.at[which, q], far_recv.at[which, q], far
         )
-    before, after, has_before, has_after = chain_peers()
-
-    first, last = (core == 0) & has_before, (core == 1) & has_after
-
-    @pl.when(first)
-    def _():
-        pl.semaphore_signal(barrier, 1, device_id=before, device_id_type=MESH)
-
-    @pl.when(last)
-    def _():
-        pl.semaphore_signal(barrier, 1, device_id=after, device_id_type=MESH)
-
-    pl.semaphore_wait(barrier, 15 + jnp.where(first | last, 1, 0))
+
+    def round_by(which, q, device):
+        return remote(
+            source_of(which, q), relay_buf.at[which], far_send.at[which, q], relay_recv.at[which], device
+        )
+
+    def onward(which):
+        return remote(
+            relay_buf.at[which], target_of(which, turn, core), relay_send.at[which], far_recv.at[which, turn], target
+        )
+
+    def start(which, q):
+        if q == 0:
+
+            @pl.when(has_far)
+            def _():
+                direct(which, q).start()
+        else:
+
+            @pl.when(has_far & jnp.logical_not(edge))
+            def _():
+                direct(which, q).start()
+
+            for edge_core in range(2):
+
+                @pl.when(on_edge(edge_core))
+                def _():
+                    round_by(which, q, relays(edge_core)[q - 1]).start()
+
+    def forward(which):
+        @pl.when(is_relay)
+        def _():
+            part = relay_buf.at[which]
+            pltpu.make_async_copy(part, part, relay_recv.at[which]).wait()
+            onward(which).start()
+
+    def arrived(which, q):
+        @pl.when(has_far)
+        def _():
+            direct(which, q).wait_recv()
+
+    def finish():
+        for which in range(2):
+            for q in range(4):
+
+                @pl.when(has_far)
+                def _():
+                    direct(which, q).wait_send()
+
+            @pl.when(is_relay)
+            def _():
+                onward(which).wait_send()
+
+    return start, forward, arrived, finish
 
 
 def remote(src, dst, send, recv, device):
@@ -98,6 +185,7 @@
     key_ref, value_ref, query_ref, dout_ref, blocks_ref, counts_ref,
     keys_out, values_out, queries_out, douts_out, lists_ref,
     blocks_vmem, counts_vmem, table_sem, send_sem, recv_sem, halo_send, halo_recv,
+    relay_buf, far_send, far_recv, relay_send, relay_recv,
 ):
     ctx, head, core, z, group = place()
     tables = [
@@ -122,66 +210,77 @@
         dst = targets[which].at[pl.ds(row, HALF), :]
         return src, dst, (group * 8 + to_z * 2 + owner_core, to_head)
 
-    order = (6, 2, 5, 7, 4, 1, 3, 0)
-    for which in range(4):
-        for turn in order:
-            src, dst, device = piece(which, turn)
-            send, recv = send_sem.at[which, turn], recv_sem.at[which, person, head]
-            if turn == 0:
-
-                @pl.when(owner_core == core)
-                def _():
-                    pltpu.make_async_copy(src, dst, recv).start()
-
-                @pl.when(owner_core != core)
-                def _():
-                    remote(src, dst, send, recv, device).start()
-            else:
-                remote(src, dst, send, recv, device).start()
+    straight, across = (2, 1, 3, 0), (6, 5, 7, 4)
+
+    def send(which, turn):
+        src, dst, device = piece(which, turn)
+        out, recv = send_sem.at[which, turn], recv_sem.at[which, person, head]
+        if turn == 0:
+
+            @pl.when(owner_core == core)
+            def _():
+                pltpu.make_async_copy(src, dst, recv).start()
+
+            @pl.when(owner_core != core)
+            def _():
+                remote(src, dst, out, recv, device).start()
+        else:
+            remote(src, dst, out, recv, device).start()
+
+    def arrive(which, who):
+        for half in range(2):
+            rows = pl.ds(pl.multiple_of(bases[which] + who * PERSON + half * HALF, HALF), HALF)
+            part = targets[which].at[rows, :]
+            pltpu.make_async_copy(part, part, recv_sem.at[which, who, half]).wait()
+
+    near, far, has_far, near_first, far_first = neighbours()
+
+    def halo(which, i):
+        src = targets[which].at[pl.ds(pl.multiple_of((2 + near_first + i) * PERSON, PERSON), PERSON), :]
+        dst = targets[which].at[pl.ds(pl.multiple_of((6 * core + i) * PERSON, PERSON), PERSON), :]
+        return remote(src, dst, halo_send.at[which, i], halo_recv.at[which, i], near)
+
+    def far_source(which, q):
+        return targets[which].at[pl.ds(pl.multiple_of((2 + far_first) * PERSON + q * HALF, HALF), HALF), :]
+
+    def far_target(which, q, to_core):
+        return targets[which].at[pl.ds(pl.multiple_of(6 * to_core * PERSON + q * HALF, HALF), HALF), :]
+
+    far_start, far_forward, far_arrived, far_finish = far_pieces(
+        far_source, far_target, relay_buf, far_send, far_recv, relay_send, relay_recv
+    )
+    for which in range(3):
+        for pair in zip(across, straight):
+            for turn in pair:
+                send(which, turn)
     for table in tables:
         table.wait()
     compact_lists(blocks_vmem, counts_vmem, lists_ref)
-    before, after, has_before, has_after = chain_peers()
-
-    def arrive(which, who):
-        for half in range(2):
-            rows = pl.ds(bases[which] + who * PERSON + half * HALF, HALF)
-            part = targets[which].at[rows, :]
-            pltpu.make_async_copy(part, part, recv_sem.at[which, who, half]).wait()
-
-    def halo(which, who):
-        target = targets[which]
-        src = target.at[pl.ds((2 + who) * PERSON, PERSON), :]
-        to = 6 + who if who < 2 else who - 2
-        dst = target.at[pl.ds(to * PERSON, PERSON), :]
-        return remote(
-            src, dst, halo_send.at[which, who], halo_recv.at[which, who], before if who < 2 else after
-        )
-
-    for which in range(2):
-        for who in range(4):
-            arrive(which, who)
-
-            @pl.when(has_before if who < 2 else has_after)
-            def _():
-                halo(which, who).start()
-
+    for which in range(2):
+        for i in range(2):
+            arrive(which, far_first + i)
+            far_start(which, 2 * i)
+            far_start(which, 2 * i + 1)
+    for pair in zip(across, straight):
+        for turn in pair:
+            send(3, turn)
+    for which in range(2):
+        for i in range(2):
+            arrive(which, near_first + i)
+            halo(which, i).start()
+        far_forward(which)
     for which in range(2, 4):
         for who in range(4):
             arrive(which, who)
     for which in range(2):
-        for who in range(4):
-
-            @pl.when(has_before if who < 2 else has_after)
-            def _():
-                halo(which, who).wait_send()
-
-            @pl.when(has_after if who < 2 else has_before)
-            def _():
-                halo(which, who).wait_recv()
-
+        for i in range(2):
+            halo(which, i).wait_send()
+            halo(which, i).wait_recv()
+        for q in range(4):
+            far_arrived(which, q)
+    far_finish()
     for which in range(4):
-        for turn in order:
+        for turn in range(8):
             src, dst, device = piece(which, turn)
             copy = remote(src, dst, send_sem.at[which, turn], recv_sem.at[which, person, head], device)
             if turn == 0:
@@ -296,41 +395,48 @@
 def exchange_out(
     dquery_ref, dkey_ref, dvalue_ref,
     dquery_out, dkey_out, dvalue_out,
-    arrived, total, send_sem, recv_sem, halo_send, halo_recv,
+    arrived, far_arrived_buf, total, send_sem, recv_sem, halo_send, halo_recv,
+    relay_buf, far_send, far_recv, relay_send, relay_recv,
 ):
     ctx, head, core, z, group = place()
     greet()
-    before, after, has_before, has_after = chain_peers()
+    near, far, has_far, near_first, far_first = neighbours()
     parts = (dkey_ref, dvalue_ref)
     outs = (dquery_out, dkey_out, dvalue_out)
 
-    def halo(which, who):
-        spot = 6 + who if who < 2 else who - 2
+    def halo(which, i):
+        spot = 6 - 6 * core + i
         return remote(
-            parts[which].at[pl.ds(spot * PERSON, PERSON), :],
-            arrived.at[which, who],
-            halo_send.at[which, who],
-            halo_recv.at[which, who],
-            after if who < 2 else before,
+            parts[which].at[pl.ds(pl.multiple_of(spot * PERSON, PERSON), PERSON), :],
+            arrived.at[which, i],
+            halo_send.at[which, i],
+            halo_recv.at[which, i],
+            near,
         )
 
-    for which in range(2):
-        for who in range(4):
-
-            @pl.when(has_after if who < 2 else has_before)
-            def _():
-                halo(which, who).start()
-
-    column = pl.multiple_of((head * 4 + z) * PAIR, PAIR)
+    def far_source(which, q):
+        return parts[which].at[pl.ds(pl.multiple_of(6 * core * PERSON + q * HALF, HALF), HALF), :]
+
+    def far_target(which, q, to_core):
+        return far_arrived_buf.at[which, pl.ds(pl.multiple_of(q * HALF, HALF), HALF), :]
+
+    far_start, far_forward, far_arrived, far_finish = far_pieces(
+        far_source, far_target, relay_buf, far_send, far_recv, relay_send, relay_recv
+    )
+    for which in range(2):
+        for q in range(4):
+            far_start(which, q)
+    for which in range(2):
+        for i in range(2):
+            halo(which, i).start()
+
+    pair = head * 4 + z
+    column = pl.multiple_of(pair * PAIR, PAIR)
 
     def piece(which, who, half):
         src = dquery_ref if which == 0 else total.at[which - 1]
-        src = src.at[pl.ds(who * PERSON + half * HALF, HALF), :]
-        dst = outs[which].at[:, pl.ds(column, PAIR)]
-        device = (group * 8 + core * 4 + who, jnp.int32(half))
-        return src, dst, device
-
-    pair = head * 4 + z
+        src = src.at[pl.ds(pl.multiple_of(who * PERSON + half * HALF, HALF), HALF), :]
+        return src, outs[which].at[:, pl.ds(column, PAIR)], (group * 8 + core * 4 + who, half)
 
     def send(which, who, half):
         src, dst, device = piece(which, who, half)
@@ -345,41 +451,53 @@
         def _():
             remote(src, dst, send_sem.at[which, who, half], recv, device).start()
 
+    def add(which, side, i):
+        who = (far_first if side else near_first) + i
+        own = parts[which][pl.ds(pl.multiple_of((2 + who) * PERSON, PERSON), PERSON), :].astype(jnp.float32)
+        rows = pl.ds(pl.multiple_of(who * PERSON, PERSON), PERSON)
+        if not side:
+            halo(which, i).wait_recv()
+            total[which, rows, :] = (own + arrived[which, i].astype(jnp.float32)).astype(jnp.bfloat16)
+            return
+        far_arrived(which, 2 * i)
+        far_arrived(which, 2 * i + 1)
+
+        @pl.when(has_far)
+        def _():
+            other = far_arrived_buf[which, pl.ds(i * PERSON, PERSON), :].astype(jnp.float32)
+            total[which, rows, :] = (own + other).astype(jnp.bfloat16)
+
+        @pl.when(jnp.logical_not(has_far))
+        def _():
+            total[which, rows, :] = own.astype(jnp.bfloat16)
+
     for who in range(4):
-        for half in range(2):
-            send(0, who, half)
-    for which in range(2):
-        for who in range(4):
-            own = parts[which][pl.ds((2 + who) * PERSON, PERSON), :].astype(jnp.float32)
-            rows = pl.ds(who * PERSON, PERSON)
-            there = has_before if who < 2 else has_after
-
-            @pl.when(there)
-            def _():
-                halo(which, who).wait_recv()
-                total[which, rows, :] = (own + arrived[which, who].astype(jnp.float32)).astype(jnp.bfloat16)
-
-            @pl.when(jnp.logical_not(there))
-            def _():
-                total[which, rows, :] = own.astype(jnp.bfloat16)
-
-            for half in range(2):
-                send(which + 1, who, half)
-
-    for which in range(2):
-        for who in range(4):
-
-            @pl.when(has_after if who < 2 else has_before)
-            def _():
-                halo(which, who).wait_send()
+        send(0, who, 1 - head)
+        send(0, who, head)
+    for which in range(2):
+        for i in range(2):
+            add(which, 0, i)
+            send(which + 1, near_first + i, 1 - head)
+            send(which + 1, near_first + i, head)
+        if which == 0:
+            far_forward(0)
+            far_forward(1)
+    for which in range(2):
+        for i in range(2):
+            add(which, 1, i)
+            send(which + 1, far_first + i, 1 - head)
+            send(which + 1, far_first + i, head)
+    far_finish()
+    for which in range(2):
+        for i in range(2):
+            halo(which, i).wait_send()
 
     for which in range(3):
         for who in range(4):
             for half in range(2):
                 src, dst, device = piece(which, who, half)
-                itself = (device[0] == ctx) & (head == half)
-
-                @pl.when(jnp.logical_not(itself))
+
+                @pl.when((device[0] != ctx) | (head != half))
                 def _():
                     remote(
                         src, dst, send_sem.at[which, who, half], recv_sem.at[which, pair], device
@@ -419,7 +537,9 @@
         scratch_shapes=[
             pltpu.VMEM((SLOTS, blocks), jnp.int32),
             pltpu.VMEM((1, blocks), jnp.int32),
-            dma((2,)), dma((4, 8)), dma((4, 4, 2)), dma((2, 4)), dma((2, 4)),
+            dma((2,)), dma((4, 8)), dma((4, 4, 2)), dma((2, 2)), dma((2, 2)),
+            pltpu.VMEM((2, HALF, PAIR), jnp.bfloat16),
+            dma((2, 4)), dma((2, 4)), dma((2,)), dma((2,)),
         ],
         compiler_params=pltpu.CompilerParams(collective_id=0, has_side_effects=True, vmem_limit_bytes=16 << 20),
         name="exchange_in",
@@ -439,9 +559,12 @@
         in_specs=[vmem] * 3,
         out_specs=(vmem,) * 3,
         scratch_shapes=[
-            pltpu.VMEM((2, 4, PERSON, PAIR), jnp.bfloat16),
+            pltpu.VMEM((2, 2, PERSON, PAIR), jnp.bfloat16),
+            pltpu.VMEM((2, 2 * PERSON, PAIR), jnp.bfloat16),
             pltpu.VMEM((2, LOCAL * PERSON, PAIR), jnp.bfloat16),
-            dma((3, 4, 2)), dma((3, 8)), dma((2, 4)), dma((2, 4)),
+            dma((3, 4, 2)), dma((3, 8)), dma((2, 2)), dma((2, 2)),
+            pltpu.VMEM((2, HALF, PAIR), jnp.bfloat16),
+            dma((2, 4)), dma((2, 4)), dma((2,)), dma((2,)),
         ],
         compiler_params=pltpu.CompilerParams(collective_id=1, has_side_effects=True, vmem_limit_bytes=16 << 20),
         name="exchange_out",

time: 80.8 us -> 79.1 us (0.979)
  Pallas kernels: 80 us -> 78.3 us
    pallas_call x1, Pallas kernels: 15 us -> 11.5 us  [on_device(): pl.pallas_call(attend, out_shape=(narrow, wide, wide), in_specs=[pl.Block...]
    pallas_call x1, Pallas kernels: 31.2 us -> 32.5 us  [on_device(): pl.pallas_call(exchange_in, out_shape=(wide, wide, narrow, narrow, jax.Sh...]
where the time goes in v3:
time: 79.1 us; the launch traced here: 78.9 us
  Pallas kernels  78.3 us (99%)
    pallas_call x1, Pallas kernels, on_device(): pl.pallas_call(exchange_out, out_shape=(rows,) * 3, in_specs=[vmem] * 3,...  33 us
    pallas_call x1, Pallas kernels, on_device(): pl.pallas_call(exchange_in, out_shape=(wide, wide, narrow, narrow, jax.Sh...  32.5 us
    pallas_call x1, Pallas kernels, on_device(): pl.pallas_call(attend, out_shape=(narrow, wide, wide), in_specs=[pl.Block...  11.5 us

profile of v3, /device:TPU:3, one launch (start us, length us, event | category | flops | bytes accessed | tf_op | source)
XLA Modules:
  0.0 78.9 jit_solution(16275977749153167093)
XLA Ops:
  0.6 32.5 %exchange_in.1 = (bf16[4096,128]{1,0:T(8,128)(2,1)S(1)}, bf16[4096,128]{1,0:T(8,128)(2,1)S(1)}, bf16[2048,128]{1,0:T(8,128)(2,1)S(1)}, bf16[2048,128]{1,0:T(8,128)(2,1)S(1)}, s32[24,128]{1,0:T(8,128)S(1)}) custom-call(bf16[256,1024]{1,0:T(8,128)(2,1)} %key_ref.1, bf16[256,1024]{1,0:T(8,128)(2,1)} %value_ref.1, bf16[256,1024]{1,0:T(8,128)(2,1)} %query_ref.1, ...), custom_call_target="tpu_custom_call" | custom-call | tf_op jit(solution)/shard_map/exchange_in/pallas_call | solution.py:532
  33.2 11.5 %attend.1 = (bf16[2048,128]{1,0:T(8,128)(2,1)S(1)}, bf16[4096,128]{1,0:T(8,128)(2,1)S(1)}, bf16[4096,128]{1,0:T(8,128)(2,1)S(1)}) custom-call(s32[24,128]{1,0:T(8,128)S(1)} %get-tuple-element.14.lists_ref, bf16[2048,128]{1,0:T(8,128)(2,1)S(1)} %get-tuple-element.15.query_ref, bf16[2048,128]{1,0:T(8,128)(2,1)S(1)} %get-tuple-element.16.dout_ref, ...), custom_call_target="tpu_custom_call" | custom-call | tf_op jit(solution)/shard_map/attend/pallas_call | solution.py:547
  44.7 33.0 %exchange_out.1 = (bf16[256,1024]{1,0:T(8,128)(2,1)S(1)}, bf16[256,1024]{1,0:T(8,128)(2,1)S(1)}, bf16[256,1024]{1,0:T(8,128)(2,1)S(1)}) custom-call(bf16[2048,128]{1,0:T(8,128)(2,1)S(1)} %get-tuple-element.19.dquery_ref, bf16[4096,128]{1,0:T(8,128)(2,1)S(1)} %get-tuple-element.20.dkey_ref, bf16[4096,128]{1,0:T(8,128)(2,1)S(1)} %get-tuple-element.21.dvalue_ref), custom_call_target="tpu_custom_call" | custom-call | tf_op jit(solution)/shard_map/exchange_out/pallas_call | solution.py:556
  77.7 1.2 %put_out.1 = (bf16[256,1024]{1,0:T(8,128)(2,1)}, bf16[256,1024]{1,0:T(8,128)(2,1)}, bf16[256,1024]{1,0:T(8,128)(2,1)}) custom-call(bf16[256,1024]{1,0:T(8,128)(2,1)S(1)} %get-tuple-element.22.dquery_ref, bf16[256,1024]{1,0:T(8,128)(2,1)S(1)} %get-tuple-element.23.dkey_ref, bf16[256,1024]{1,0:T(8,128)(2,1)S(1)} %get-tuple-element.24.dvalue_ref), custom_call_target="tpu_custom_call" | custom-call | tf_op jit(solution)/shard_map/put_out/pallas_call | solution.py:572

commit v4 on v3

--- a/solution.py
+++ b/solution.py
@@ -15,7 +15,7 @@
 SLOTS = 16
 QBLOCKS = 32
 LIST_ROWS = 24
-STEP = 4
+STEP = 2
 GROUPS = 8
 GROUP = 2
 MESH = pl.DeviceIdType.MESH
@@ -261,14 +261,30 @@
             arrive(which, far_first + i)
             far_start(which, 2 * i)
             far_start(which, 2 * i + 1)
-    for pair in zip(across, straight):
-        for turn in pair:
+    passes_on = relay_role()[0]
+
+    @pl.when(jnp.logical_not(passes_on))
+    def _():
+        for pair in zip(across, straight):
+            for turn in pair:
+                send(3, turn)
+
+    @pl.when(passes_on)
+    def _():
+        for turn in straight:
             send(3, turn)
+
     for which in range(2):
         for i in range(2):
             arrive(which, near_first + i)
             halo(which, i).start()
         far_forward(which)
+
+    @pl.when(passes_on)
+    def _():
+        for turn in across:
+            send(3, turn)
+
     for which in range(2, 4):
         for who in range(4):
             arrive(which, who)
@@ -471,17 +487,26 @@
         def _():
             total[which, rows, :] = own.astype(jnp.bfloat16)
 
+    passes_on = relay_role()[0]
+
+    def key_across():
+        for i in range(2):
+            send(1, near_first + i, 1 - head)
+
     for who in range(4):
         send(0, who, 1 - head)
         send(0, who, head)
-    for which in range(2):
-        for i in range(2):
-            add(which, 0, i)
-            send(which + 1, near_first + i, 1 - head)
-            send(which + 1, near_first + i, head)
-        if which == 0:
-            far_forward(0)
-            far_forward(1)
+    for i in range(2):
+        add(0, 0, i)
+        send(1, near_first + i, head)
+    pl.when(jnp.logical_not(passes_on))(key_across)
+    for which in range(2):
+        far_forward(which)
+    pl.when(passes_on)(key_across)
+    for i in range(2):
+        add(1, 0, i)
+        send(2, near_first + i, 1 - head)
+        send(2, near_first + i, head)
     for which in range(2):
         for i in range(2):
             add(which, 1, i)

time: 79.1 us -> 76.7 us (0.970)
  Pallas kernels: 78.3 us -> 75.9 us
    pallas_call x1, Pallas kernels: 33 us -> 29.2 us  [on_device(): pl.pallas_call(exchange_out, out_shape=(rows,) * 3, in_specs=[vmem] * 3,...]
    pallas_call x1, Pallas kernels: 11.5 us -> 12.9 us  [on_device(): pl.pallas_call(attend, out_shape=(narrow, wide, wide), in_specs=[pl.Block...]
where the time goes in v4:
time: 76.7 us; the launch traced here: 76.5 us
  Pallas kernels  75.9 us (99%)
    pallas_call x1, Pallas kernels, on_device(): pl.pallas_call(exchange_in, out_shape=(wide, wide, narrow, narrow, jax.Sh...  32.5 us
    pallas_call x1, Pallas kernels, on_device(): pl.pallas_call(exchange_out, out_shape=(rows,) * 3, in_specs=[vmem] * 3,...  29.2 us
    pallas_call x1, Pallas kernels, on_device(): pl.pallas_call(attend, out_shape=(narrow, wide, wide), in_specs=[pl.Block...  12.9 us

profile of v4, /device:TPU:3, one launch (start us, length us, event | category | flops | bytes accessed | tf_op | source)
XLA Modules:
  0.0 76.5 jit_solution(13566954553876458456)
XLA Ops:
  0.6 32.5 %exchange_in.1 = (bf16[4096,128]{1,0:T(8,128)(2,1)S(1)}, bf16[4096,128]{1,0:T(8,128)(2,1)S(1)}, bf16[2048,128]{1,0:T(8,128)(2,1)S(1)}, bf16[2048,128]{1,0:T(8,128)(2,1)S(1)}, s32[24,128]{1,0:T(8,128)S(1)}) custom-call(bf16[256,1024]{1,0:T(8,128)(2,1)} %key_ref.1, bf16[256,1024]{1,0:T(8,128)(2,1)} %value_ref.1, bf16[256,1024]{1,0:T(8,128)(2,1)} %query_ref.1, ...), custom_call_target="tpu_custom_call" | custom-call | tf_op jit(solution)/shard_map/exchange_in/pallas_call | solution.py:557
  33.2 12.9 %attend.1 = (bf16[2048,128]{1,0:T(8,128)(2,1)S(1)}, bf16[4096,128]{1,0:T(8,128)(2,1)S(1)}, bf16[4096,128]{1,0:T(8,128)(2,1)S(1)}) custom-call(s32[24,128]{1,0:T(8,128)S(1)} %get-tuple-element.14.lists_ref, bf16[2048,128]{1,0:T(8,128)(2,1)S(1)} %get-tuple-element.15.query_ref, bf16[2048,128]{1,0:T(8,128)(2,1)S(1)} %get-tuple-element.16.dout_ref, ...), custom_call_target="tpu_custom_call" | custom-call | tf_op jit(solution)/shard_map/attend/pallas_call | solution.py:572
  46.1 29.2 %exchange_out.1 = (bf16[256,1024]{1,0:T(8,128)(2,1)S(1)}, bf16[256,1024]{1,0:T(8,128)(2,1)S(1)}, bf16[256,1024]{1,0:T(8,128)(2,1)S(1)}) custom-call(bf16[2048,128]{1,0:T(8,128)(2,1)S(1)} %get-tuple-element.19.dquery_ref, bf16[4096,128]{1,0:T(8,128)(2,1)S(1)} %get-tuple-element.20.dkey_ref, bf16[4096,128]{1,0:T(8,128)(2,1)S(1)} %get-tuple-element.21.dvalue_ref), custom_call_target="tpu_custom_call" | custom-call | tf_op jit(solution)/shard_map/exchange_out/pallas_call | solution.py:581
  75.3 1.2 %put_out.1 = (bf16[256,1024]{1,0:T(8,128)(2,1)}, bf16[256,1024]{1,0:T(8,128)(2,1)}, bf16[256,1024]{1,0:T(8,128)(2,1)}) custom-call(bf16[256,1024]{1,0:T(8,128)(2,1)S(1)} %get-tuple-element.22.dquery_ref, bf16[256,1024]{1,0:T(8,128)(2,1)S(1)} %get-tuple-element.23.dkey_ref, bf16[256,1024]{1,0:T(8,128)(2,1)S(1)} %get-tuple-element.24.dvalue_ref), custom_call_target="tpu_custom_call" | custom-call | tf_op jit(solution)/shard_map/put_out/pallas_call | solution.py:597

commit v5 on v4

--- a/solution.py
+++ b/solution.py
@@ -55,7 +55,7 @@
     return turn < 3, turn + 1, target, other
 
 
-def greet():
+def greet(meanwhile=None):
     ctx, head, core, z, group = place()
     barrier = pltpu.get_barrier_semaphore()
 
@@ -77,6 +77,8 @@
     def _():
         hello(other)
 
+    if meanwhile is not None:
+        meanwhile()
     count = 15 + jnp.where(has_far, 1, 0) + jnp.where(edge, 3, 0)
     pl.semaphore_wait(barrier, count)
 
@@ -183,7 +185,7 @@
 
 def exchange_in(
     key_ref, value_ref, query_ref, dout_ref, blocks_ref, counts_ref,
-    keys_out, values_out, queries_out, douts_out, lists_ref,
+    keys_out, values_out, queries_out, douts_out, lists_ref, dkey_zero, dvalue_zero,
     blocks_vmem, counts_vmem, table_sem, send_sem, recv_sem, halo_send, halo_recv,
     relay_buf, far_send, far_recv, relay_send, relay_recv,
 ):
@@ -256,6 +258,13 @@
     for table in tables:
         table.wait()
     compact_lists(blocks_vmem, counts_vmem, lists_ref)
+
+    @pl.loop(0, WINDOW)
+    def _(chunk):
+        rows = pl.ds(pl.multiple_of(chunk * PERSON, PERSON), PERSON)
+        dkey_zero[rows, :] = jnp.zeros((PERSON, PAIR), jnp.float32)
+        dvalue_zero[rows, :] = jnp.zeros((PERSON, PAIR), jnp.float32)
+
     for which in range(2):
         for i in range(2):
             arrive(which, far_first + i)
@@ -309,16 +318,8 @@
 
 
 def attend(
-    lists_ref, query_ref, dout_ref, key_ref, value_ref, dquery_ref, dkey_ref, dvalue_ref, dkey_sum, dvalue_sum
+    lists_ref, query_ref, dout_ref, key_ref, value_ref, dkey_zero, dvalue_zero, dquery_ref, dkey_sum, dvalue_sum
 ):
-    rows_all = WINDOW * PERSON
-
-    @pl.loop(0, rows_all // PERSON)
-    def _(chunk):
-        rows = pl.ds(pl.multiple_of(chunk * PERSON, PERSON), PERSON)
-        dkey_sum[rows, :] = jnp.zeros((PERSON, PAIR), jnp.float32)
-        dvalue_sum[rows, :] = jnp.zeros((PERSON, PAIR), jnp.float32)
-
     first_head = lax.broadcasted_iota(jnp.int32, (BLOCK, PAIR), 1) < HEAD_DIM
     scale = HEAD_DIM ** (-0.5)
     nt = (((1,), (1,)), ((), ()))
@@ -401,29 +402,30 @@
             def _():
                 body(group, width)
 
-    @pl.loop(0, rows_all // PERSON)
-    def _(chunk):
-        rows = pl.ds(pl.multiple_of(chunk * PERSON, PERSON), PERSON)
-        dkey_ref[rows, :] = dkey_sum[rows, :].astype(jnp.bfloat16)
-        dvalue_ref[rows, :] = dvalue_sum[rows, :].astype(jnp.bfloat16)
-
 
 def exchange_out(
     dquery_ref, dkey_ref, dvalue_ref,
     dquery_out, dkey_out, dvalue_out,
-    arrived, far_arrived_buf, total, send_sem, recv_sem, halo_send, halo_recv,
+    rounded, arrived, far_arrived_buf, total, send_sem, recv_sem, halo_send, halo_recv,
     relay_buf, far_send, far_recv, relay_send, relay_recv,
 ):
     ctx, head, core, z, group = place()
-    greet()
     near, far, has_far, near_first, far_first = neighbours()
     parts = (dkey_ref, dvalue_ref)
+
+    def round_halo():
+        for which in range(2):
+            for side in range(2):
+                rows = pl.ds(6 * side * PERSON, 2 * PERSON)
+                rounded[which, pl.ds(2 * side * PERSON, 2 * PERSON), :] = parts[which][rows, :].astype(jnp.bfloat16)
+
+    greet(round_halo)
     outs = (dquery_out, dkey_out, dvalue_out)
 
     def halo(which, i):
-        spot = 6 - 6 * core + i
+        spot = 2 - 2 * core + i
         return remote(
-            parts[which].at[pl.ds(pl.multiple_of(spot * PERSON, PERSON), PERSON), :],
+            rounded.at[which, pl.ds(pl.multiple_of(spot * PERSON, PERSON), PERSON), :],
             arrived.at[which, i],
             halo_send.at[which, i],
             halo_recv.at[which, i],
@@ -431,7 +433,7 @@
         )
 
     def far_source(which, q):
-        return parts[which].at[pl.ds(pl.multiple_of(6 * core * PERSON + q * HALF, HALF), HALF), :]
+        return rounded.at[which, pl.ds(pl.multiple_of(2 * core * PERSON + q * HALF, HALF), HALF), :]
 
     def far_target(which, q, to_core):
         return far_arrived_buf.at[which, pl.ds(pl.multiple_of(q * HALF, HALF), HALF), :]
@@ -469,7 +471,7 @@
 
     def add(which, side, i):
         who = (far_first if side else near_first) + i
-        own = parts[which][pl.ds(pl.multiple_of((2 + who) * PERSON, PERSON), PERSON), :].astype(jnp.float32)
+        own = parts[which][pl.ds(pl.multiple_of((2 + who) * PERSON, PERSON), PERSON), :]
         rows = pl.ds(pl.multiple_of(who * PERSON, PERSON), PERSON)
         if not side:
             halo(which, i).wait_recv()
@@ -503,15 +505,18 @@
     for which in range(2):
         far_forward(which)
     pl.when(passes_on)(key_across)
+    def far_part(which):
+        for i in range(2):
+            add(which, 1, i)
+            send(which + 1, far_first + i, 1 - head)
+            send(which + 1, far_first + i, head)
+
+    far_part(0)
     for i in range(2):
         add(1, 0, i)
         send(2, near_first + i, 1 - head)
         send(2, near_first + i, head)
-    for which in range(2):
-        for i in range(2):
-            add(which, 1, i)
-            send(which + 1, far_first + i, 1 - head)
-            send(which + 1, far_first + i, head)
+    far_part(1)
     far_finish()
     for which in range(2):
         for i in range(2):
@@ -554,11 +559,12 @@
     sources = [
         pltpu.with_memory_space_constraint(x, pltpu.HBM) for x in (keys_in, values, queries, d_out) + tables
     ]
-    keys, vals, query, dout, lists = pl.pallas_call(
+    sums = jax.ShapeDtypeStruct((WINDOW * PERSON, PAIR), jnp.float32)
+    keys, vals, query, dout, lists, key_sum, value_sum = pl.pallas_call(
         exchange_in,
-        out_shape=(wide, wide, narrow, narrow, jax.ShapeDtypeStruct((LIST_ROWS, 128), jnp.int32)),
+        out_shape=(wide, wide, narrow, narrow, jax.ShapeDtypeStruct((LIST_ROWS, 128), jnp.int32), sums, sums),
         in_specs=[hbm] * 6,
-        out_specs=(vmem,) * 5,
+        out_specs=(vmem,) * 7,
         scratch_shapes=[
             pltpu.VMEM((SLOTS, blocks), jnp.int32),
             pltpu.VMEM((1, blocks), jnp.int32),
@@ -571,19 +577,20 @@
     )(*sources)
     d_query, d_key, d_value = pl.pallas_call(
         attend,
-        out_shape=(narrow, wide, wide),
-        in_specs=[pl.BlockSpec(memory_space=pltpu.SMEM)] + [vmem] * 4,
+        out_shape=(narrow, sums, sums),
+        in_specs=[pl.BlockSpec(memory_space=pltpu.SMEM)] + [vmem] * 6,
         out_specs=(vmem,) * 3,
-        scratch_shapes=[pltpu.VMEM((WINDOW * PERSON, PAIR), jnp.float32)] * 2,
+        input_output_aliases={5: 1, 6: 2},
         compiler_params=pltpu.CompilerParams(vmem_limit_bytes=24 << 20),
         name="attend",
-    )(lists, query, dout, keys, vals)
+    )(lists, query, dout, keys, vals, key_sum, value_sum)
     results = pl.pallas_call(
         exchange_out,
         out_shape=(rows,) * 3,
         in_specs=[vmem] * 3,
         out_specs=(vmem,) * 3,
         scratch_shapes=[
+            pltpu.VMEM((2, 4 * PERSON, PAIR), jnp.bfloat16),
             pltpu.VMEM((2, 2, PERSON, PAIR), jnp.bfloat16),
             pltpu.VMEM((2, 2 * PERSON, PAIR), jnp.bfloat16),
             pltpu.VMEM((2, LOCAL * PERSON, PAIR), jnp.bfloat16),

time: 76.7 us -> 77.3 us (level)
  Pallas kernels: 75.9 us -> 76.8 us
    pallas_call x1, Pallas kernels: 12.9 us -> 14.1 us  [on_device(): pl.pallas_call(attend, out_shape=(narrow, sums, sums), in_specs=[pl.Block...]
where the time goes in v5:
time: 77.3 us; the launch traced here: 77.4 us
  Pallas kernels  76.8 us (99%)
    pallas_call x1, Pallas kernels, on_device(): pl.pallas_call(exchange_in, out_shape=(wide, wide, narrow, narrow, jax.Sh...  32.5 us
    pallas_call x1, Pallas kernels, on_device(): pl.pallas_call(exchange_out, out_shape=(rows,) * 3, in_specs=[vmem] * 3,...  29 us
    pallas_call x1, Pallas kernels, on_device(): pl.pallas_call(attend, out_shape=(narrow, sums, sums), in_specs=[pl.Block...  14.1 us

profile of v5, /device:TPU:3, one launch (start us, length us, event | category | flops | bytes accessed | tf_op | source)
XLA Modules:
  0.0 77.4 jit_solution(17481621731162288138)
XLA Ops:
  0.6 32.5 %exchange_in.1 = (bf16[4096,128]{1,0:T(8,128)(2,1)S(1)}, bf16[4096,128]{1,0:T(8,128)(2,1)S(1)}, bf16[2048,128]{1,0:T(8,128)(2,1)S(1)}, bf16[2048,128]{1,0:T(8,12...) custom-call(bf16[256,1024]{1,0:T(8,128)(2,1)} %key_ref.1, ...), custom_call_target="tpu_custom_call" | custom-call | tf_op jit(solution)/shard_map/exchange_in/pallas_call | solution.py:563
  33.2 14.1 %attend.1 = (bf16[2048,128]{1,0:T(8,128)(2,1)S(1)}, f32[4096,128]{1,0:T(8,128)S(1)}, f32[4096,128]{1,0:T(8,128)S(1)}) custom-call(s32[24,128]{1,0:T(8,128)S(1)} %get-tuple-element.16.lists_ref, bf16[2048,128]{1,0:T(8,128)(2,1)S(1)} %get-tuple-element.17.query_ref, ...), custom_call_target="tpu_custom_call", output_to_operand_aliasing={{1}: (5, {}), {2}: (6, {})} | custom-call | tf_op jit(solution)/shard_map/attend/pallas_call | solution.py:578
  47.3 29.0 %exchange_out.1 = (bf16[256,1024]{1,0:T(8,128)(2,1)S(1)}, bf16[256,1024]{1,0:T(8,128)(2,1)S(1)}, bf16[256,1024]{1,0:T(8,128)(2,1)S(1)}) custom-call(bf16[2048,128]{1,0:T(8,128)(2,1)S(1)} %get-tuple-element.23.dquery_ref, f32[4096,128]{1,0:T(8,128)S(1)} %get-tuple-element.24.dkey_ref, f32[4096,128]{1,0:T(8,128)S(1)} %get-tuple-element.25.dvalue_ref), custom_call_target="tpu_custom_call" | custom-call | tf_op jit(solution)/shard_map/exchange_out/pallas_call | solution.py:587
  76.3 1.2 %put_out.1 = (bf16[256,1024]{1,0:T(8,128)(2,1)}, bf16[256,1024]{1,0:T(8,128)(2,1)}, bf16[256,1024]{1,0:T(8,128)(2,1)}) custom-call(bf16[256,1024]{1,0:T(8,128)(2,1)S(1)} %get-tuple-element.26.dquery_ref, bf16[256,1024]{1,0:T(8,128)(2,1)S(1)} %get-tuple-element.27.dkey_ref, bf16[256,1024]{1,0:T(8,128)(2,1)S(1)} %get-tuple-element.28.dvalue_ref), custom_call_target="tpu_custom_call" | custom-call | tf_op jit(solution)/shard_map/put_out/pallas_call | solution.py:604
